TPU v7x, 256 devices: a whole 4x4x8 slice. The times are simulated.
256 devices in a mesh: ctx: 64 (over y, z, core), head: 4 (over x).
Axes of the slice: x: 4, y: 4, z: 8, core: 2. Of those that a mesh axis runs over, the one named last changes fastest.
Arguments:
- tokens: bfloat16 [32768, 1024], P(('ctx', 'head')), may hold values from -6 to 6
- conv_kernel: float32 [7, 1024], replicated, may hold values from -2.5 to 2.5
- w_qkv: bfloat16 [1024, 3072], replicated, may hold values from -0.1875 to 0.1875
- w_out: bfloat16 [1024, 1024], replicated, may hold values from -0.1875 to 0.1875
- lengths: int32 [32], replicated, may hold values from 1 to 2048, 32768 in all
- cotangent: bfloat16 [32768, 1024], P(('ctx', 'head')), may hold values from -6 to 6
Outputs:
- attended: bfloat16 [32768, 1024], P(('ctx', 'head'))
- input_grad: bfloat16 [32768, 1024], P(('ctx', 'head'))
Inputs may be any that keep to these rules, and one draw needn't show every extreme that they name: `lengths`: they sum to 32768; the longest recording has exactly 2048 tokens.
All inputs are finite; a program needn't handle non-finite values.
Results may differ from a plain program's by a relative error of at most 0.017.
The roundings to bfloat16 on the way count: a program that leaves them out, or rounds other values in their place, can miss the bound.
Values may be sent and summed in bfloat16 or wider, within the bound.
A program may use at most 128 MiB of HBM per device.

v0:
```python
import functools
import math

import jax
import jax.numpy as jnp
from jax import lax
from jax.experimental import pallas as pl
from jax.experimental.pallas import tpu as pltpu
from jax.sharding import PartitionSpec as P

HD = 64
KS = 7
HALO = 16
OWN, PREV, PREVX, PAIR = 0, 1, 2, 3
MESH = pl.DeviceIdType.MESH
F32, BF16, I32 = jnp.float32, jnp.bfloat16, jnp.int32


def nt(a, b):
    return lax.dot_general(a, b, (((1,), (1,)), ((), ())), preferred_element_type=F32)


def nn(a, b):
    return jnp.dot(a, b, preferred_element_type=F32)


def layer_kernel(
    n_ctx,
    tok_hbm,
    cot_hbm,
    wqkv_hbm,
    wout_hbm,
    convk,
    lens,
    att_out,
    ig_out,
    ext,
    ext32,
    cmask,
    cot,
    w3,
    wout,
    mixed,
    kvs,
    qs,
    ds_,
    kv,
    q,
    do,
    kt,
    vt,
    qm,
    dm,
    starts,
    e_ref,
    ot,
    tot,
    of_s,
    of_r,
    tf_s,
    tf_r,
    stat,
    st_s,
    ctxt,
    cxs,
    cx,
    dkv,
    dqt,
    pp_s,
    pp_r,
    sp_s,
    sp_r,
    ps_s,
    ps_r,
    dqf_s,
    dqf_r,
    gs,
    g,
    gm,
    ld,
    s_h,
    r_h,
    s_kv,
    r_kv,
    s_z,
    r_z,
    s_sp,
    r_sp,
    s_pp,
    r_pp,
    s_q,
    r_q,
    s_d,
    r_d,
    s_f,
    r_f,
    s_cx,
    r_cx,
    s_gr,
    r_gr,
    s_g,
    r_g,
):
    c, x = lax.axis_index("ctx"), lax.axis_index("head")
    core = lax.rem(c, 2)
    ahead = lax.rem(c + 2, n_ctx)
    behind = lax.rem(c + n_ctx - 2, n_ctx)
    pair = c + 1 - 2 * core
    rows, width = 128, 256
    seq = 512
    nx = 4
    model = 1024

    up_x = lax.rem(x + 1, nx)
    up_c = lax.rem(c + (x + 1) // nx, n_ctx)
    dn_x = lax.rem(x + nx - 1, nx)
    dn_c = lax.rem(c + n_ctx - (nx - x) // nx, n_ctx)

    loads = [
        pltpu.make_async_copy(tok_hbm, ext.at[pl.ds(HALO, rows), :], ld.at[0]),
        pltpu.make_async_copy(cot_hbm, cot, ld.at[1]),
        pltpu.make_async_copy(wout_hbm, wout, ld.at[2]),
        pltpu.make_async_copy(wqkv_hbm.at[:, pl.ds(model, model)], w3.at[1], ld.at[3]),
        pltpu.make_async_copy(wqkv_hbm.at[:, pl.ds(2 * model, model)], w3.at[2], ld.at[4]),
        pltpu.make_async_copy(wqkv_hbm.at[:, pl.ds(0, model)], w3.at[0], ld.at[5]),
    ]
    for i in (0, 3, 4, 5, 1, 2):
        loads[i].start()

    barrier = pltpu.get_barrier_semaphore()
    peers = [(c, lax.rem(x + d, nx)) for d in (1, 2, 3)]
    peers += [(ahead, x), (behind, x), (pair, x), (up_c, up_x), (dn_c, dn_x)]
    for peer in peers:
        pl.semaphore_signal(barrier, inc=1, device_id=peer, device_id_type=MESH)
    pl.semaphore_wait(barrier, len(peers))

    def send(src, dst, ss, rs, peer):
        copy = pltpu.make_async_remote_copy(
            src_ref=src, dst_ref=dst, send_sem=ss, recv_sem=rs, device_id=peer, device_id_type=MESH
        )
        copy.start()
        return copy

    pending = []

    loads[0].wait()
    h_up = send(ext.at[pl.ds(rows, HALO), :], ext.at[pl.ds(0, HALO), :], s_h.at[0], r_h.at[0], (up_c, up_x))
    h_dn = send(
        ext.at[pl.ds(HALO, HALO), :], ext.at[pl.ds(HALO + rows, HALO), :], s_h.at[1], r_h.at[1], (dn_c, dn_x)
    )

    ends = []
    run = jnp.int32(0)
    for i in range(lens.shape[0]):
        run = run + lens[i]
        ends.append(run)
    lane = lax.broadcasted_iota(I32, (8, seq), 1)
    for qi, shard in ((0, c), (1, ahead)):
        pos = shard * seq + lane
        first = jnp.zeros((8, seq), I32)
        for end in ends:
            first = jnp.where(pos >= end, end, first)
        starts[qi] = first
    row_pos = (c * nx + x) * rows + lax.broadcasted_iota(I32, (rows, 128), 0)
    first = jnp.zeros((rows, 128), I32)
    for end in ends:
        first = jnp.where(row_pos >= end, end, first)
    last = jnp.zeros((rows, 128), I32)
    for end in reversed(ends):
        last = jnp.where(row_pos < end, end, last)
    for t in range(KS):
        near = row_pos + (t - KS // 2)
        cmask[t] = jnp.where((near >= first) & (near < last), 1.0, 0.0).astype(F32)

    def convolve(out, flip):
        def chunk(i, carry):
            lanes = pl.ds(pl.multiple_of(i * 128, 128), 128)
            acc = ext32[pl.ds(HALO, rows), lanes]
            for t in range(KS):
                tap = convk[pl.ds(KS - 1 - t if flip else t, 1), lanes]
                acc = acc + tap * ext32[pl.ds(HALO - KS // 2 + t, rows), lanes] * cmask[t]
            out[:, lanes] = acc.astype(BF16)
            return carry

        lax.fori_loop(0, model // 128, chunk, 0)

    h_up.wait()
    h_dn.wait()
    ext32[...] = ext[...].astype(F32)
    convolve(mixed, False)

    loads[3].wait()
    loads[4].wait()
    kv_sends = []
    for d in (2, 1, 3, 0):
        p = lax.rem(x + d, nx)
        cols = pl.ds(pl.multiple_of(p * width, width), width)
        for part in (0, 1):
            block = nn(mixed[...], w3[1 + part, :, cols]).astype(BF16)
            kvs[d, :, part * width : (part + 1) * width] = block
        if d:
            kv_sends.append(
                (d, send(kvs.at[d], kv.at[OWN, pl.ds(pl.multiple_of(x * rows, rows), rows), :], s_kv.at[d], r_kv.at[d], (c, p)))
            )
        else:
            kv[OWN, pl.ds(pl.multiple_of(x * rows, rows), rows), :] = kvs[0]

    def piece(d):
        return pl.ds(pl.multiple_of(lax.rem(x + nx - d, nx) * rows, rows), rows)

    z_sends, sp_sends = {}, {}

    def forward(d):
        at = piece(d)
        z_sends[d] = send(kv.at[OWN, at, :], kv.at[PREV, at, :], s_z.at[d], r_z.at[d], (ahead, x))
        sp_sends[d] = send(kv.at[OWN, at, :], kv.at[PAIR, at, :], s_sp.at[d], r_sp.at[d], (pair, x))

    forward(0)

    loads[5].wait()
    q_sends = []
    for d in (2, 1, 3, 0):
        p = lax.rem(x + d, nx)
        cols = pl.ds(pl.multiple_of(p * width, width), width)
        block = nn(mixed[...], w3[0, :, cols]).astype(BF16)
        if d:
            qs[d] = block
            q_sends.append(
                send(qs.at[d], q.at[0, pl.ds(pl.multiple_of(x * rows, rows), rows), :], s_q.at[d], r_q.at[d], (c, p))
            )
        else:
            q[0, pl.ds(pl.multiple_of(x * rows, rows), rows), :] = block

    loads[1].wait()
    loads[2].wait()
    d_sends = []
    for d in (2, 1, 3, 0):
        p = lax.rem(x + d, nx)
        cols = pl.ds(pl.multiple_of(p * width, width), width)
        block = nt(cot[...], wout[cols, :]).astype(BF16)
        if d:
            ds_[d] = block
            d_sends.append(
                send(ds_.at[d], do.at[0, pl.ds(pl.multiple_of(x * rows, rows), rows), :], s_d.at[d], r_d.at[d], (c, p))
            )
        else:
            do[0, pl.ds(pl.multiple_of(x * rows, rows), rows), :] = block

    for d, copy in sorted(kv_sends, key=lambda item: (1, 3, 2).index(item[0])):
        copy.wait_recv()
        forward(d)
    for copy in q_sends:
        copy.wait_recv()
    qf = send(q.at[0], q.at[1], s_f.at[0], r_f.at[0], (behind, x))
    for copy in d_sends:
        copy.wait_recv()
    df = send(do.at[0], do.at[1], s_f.at[1], r_f.at[1], (behind, x))
    for _, copy in kv_sends:
        copy.wait_send()
    for copy in q_sends + d_sends:
        copy.wait_send()

    half = lax.broadcasted_iota(I32, (seq, 128), 1) // HD

    def split_heads(src, dst, qi):
        for h in range(4):
            block = src[qi, :, (h // 2) * 128 : (h // 2) * 128 + 128].astype(F32)
            dst[qi, h] = jnp.where(half == h % 2, block, 0.0).astype(BF16)

    def turn(slot):
        kt[slot] = kv[slot, :, 0:width].astype(F32).T.astype(BF16)
        vt[slot] = kv[slot, :, width : 2 * width].astype(F32).T.astype(BF16)

    ot[...] = jnp.zeros_like(ot)
    tot[...] = jnp.zeros_like(tot)
    dqt[...] = jnp.zeros_like(dqt)
    dkv[...] = jnp.zeros_like(dkv)

    scale = HD ** -0.5
    scale2 = scale * math.log2(math.e)
    kc = 256
    k_iota = lax.broadcasted_iota(I32, (kc, seq), 0)
    q_iota = lax.broadcasted_iota(I32, (kc, seq), 1)

    def attend(block, qi, slot, distance, diag=False):
        def step(i, carry):
            hp, part = i // 2, lax.rem(i, 2)
            k0 = pl.multiple_of(part * kc, kc)
            lanes = pl.ds(pl.multiple_of(hp * 128, 128), 128)
            keys = kv[slot, pl.ds(k0, kc), lanes]
            q_shard = jnp.where(qi == 0, c, ahead)
            k_pos = (q_shard - distance) * seq + k0 + k_iota
            ok = k_pos >= starts[qi, 0:1, :]
            if diag:
                ok = ok & (k0 + k_iota <= q_iota)
            for s in (0, 1):
                h = hp * 2 + s
                score = nt(keys, qm[qi, h])
                e = jnp.where(ok, jnp.exp2(score * scale2), 0.0)
                e_ref[block, h, pl.ds(k0, kc), :] = e
                tot[qi, h] += jnp.sum(e, axis=0, keepdims=True)
                head_rows = pl.ds(pl.multiple_of(h * HD, HD), HD)
                ot[qi, head_rows, :] += nn(vt[slot, head_rows, pl.ds(k0, kc)], e.astype(BF16))
            return carry

        lax.fori_loop(0, 4, step, 0)

    def grads(block, qi, slot, hp):
        lanes = pl.ds(hp * 128, 128)

        def step(part, carry):
            k0 = pl.multiple_of(part * kc, kc)
            values = kv[slot, pl.ds(k0, kc), pl.ds(width + hp * 128, 128)]
            for s in (0, 1):
                h = hp * 2 + s
                prob = e_ref[block, h, pl.ds(k0, kc), :] * stat[qi, h : h + 1, :]
                d_prob = nt(values, dm[qi, h])
                d_score = (prob * (d_prob - stat[qi, 4 + h : 5 + h, :])).astype(BF16)
                dkv[slot, hp, pl.ds(k0, kc), 128:256] += nn(prob.astype(BF16), dm[qi, h])
                dkv[slot, hp, pl.ds(k0, kc), 0:128] += nn(d_score, qm[qi, h])
                head_rows = pl.ds(h * HD, HD)
                dqt[qi, head_rows, :] += nn(kt[slot, head_rows, pl.ds(k0, kc)], d_score)
            return carry

        lax.fori_loop(0, seq // kc, step, 0)

    split_heads(q, qm, 0)
    turn(OWN)
    attend(0, 0, OWN, 0, diag=True)
    pp_sends = {}
    for d in (0, 1, 3, 2):
        z_sends[d].wait_recv()
        at = piece(d)
        pp_sends[d] = send(kv.at[PREV, at, :], kv.at[PREVX, at, :], s_pp.at[d], r_pp.at[d], (pair, x))
    qf.wait_recv()
    split_heads(q, qm, 1)
    turn(PREV)

    def near_far(qi, carry):
        attend(1 + qi, qi, PREV, 2 + 2 * qi)
        return carry

    lax.fori_loop(0, 2, near_far, 0)
    for d in range(nx):
        pp_sends[d].wait_recv()
        sp_sends[d].wait_recv()
    turn(PREVX)
    turn(PAIR)
    far = 1 - core
    far_slot = PREVX + core

    def crossed(j, carry):
        attend(3 + j, j * far, PREVX + j * core, jnp.where(j == 0, 1 + 2 * core, 3 - 2 * core))
        return carry

    lax.fori_loop(0, 2, crossed, 0)
    of_s[...] = ot[1].astype(BF16)
    for h in range(4):
        tf_s[h : h + 1, :] = tot[1, h]
        tf_s[4 + h : 5 + h, :] = tot[1, h]
    of = send(of_s, of_r, s_f.at[2], r_f.at[2], (ahead, x))
    tf = send(tf_s, tf_r, s_f.at[3], r_f.at[3], (ahead, x))
    df.wait_recv()
    split_heads(do, dm, 0)
    split_heads(do, dm, 1)
    tf.wait_recv()
    of.wait_recv()

    for h in range(4):
        head_rows = slice(h * HD, (h + 1) * HD)
        total = tot[0, h] + tf_r[h : h + 1, :]
        inverse = 1.0 / total
        context = ((ot[0, head_rows, :] + of_r[head_rows, :].astype(F32)) / total).astype(BF16)
        ctxt[head_rows, :] = context.astype(F32)
        stat[0, h : h + 1, :] = inverse
    d_turned = do[0].astype(F32).T
    product = d_turned * ctxt[...]
    for h in range(4):
        stat[0, 4 + h : 5 + h, :] = jnp.sum(product[h * HD : (h + 1) * HD, :], axis=0, keepdims=True)
    st_s[...] = stat[0]
    st = send(st_s, stat.at[1], s_f.at[4], r_f.at[4], (behind, x))
    cx_sends = []
    for d in (2, 1, 3, 0):
        p = lax.rem(x + d, nx)
        block = ctxt[:, pl.ds(pl.multiple_of(p * rows, rows), rows)].T.astype(BF16)
        if d:
            cxs[d] = block
            cx_sends.append(send(cxs.at[d], cx.at[x], s_cx.at[d], r_cx.at[d], (c, p)))
        else:
            cx[x] = block
    st.wait_recv()

    sent = []
    for hp in (0, 1):

        def crossed_grads(j, carry):
            grads(3 + j, j * far, PREVX + j * core, hp)
            return carry

        lax.fori_loop(0, 2, crossed_grads, 0)
        pp_s[hp] = dkv[PREVX, hp].astype(BF16)
        ppg = send(pp_s.at[hp], pp_r.at[hp], s_gr.at[hp], r_gr.at[hp], (pair, x))
        sp_s[hp] = dkv[PAIR, hp].astype(BF16)
        spg = send(sp_s.at[hp], sp_r.at[hp], s_gr.at[2 + hp], r_gr.at[2 + hp], (pair, x))

        def near_far_grads(qi, carry):
            grads(1 + qi, qi, PREV, hp)
            return carry

        lax.fori_loop(0, 2, near_far_grads, 0)
        dq_rows = pl.ds(hp * 128, 128)
        dqf_s[dq_rows, :] = dqt[1, dq_rows, :].astype(BF16)
        dqf = send(dqf_s.at[dq_rows, :], dqf_r.at[dq_rows, :], s_gr.at[6 + hp], r_gr.at[6 + hp], (ahead, x))
        ppg.wait_recv()
        ps_s[hp] = (dkv[PREV, hp] + pp_r[hp].astype(F32)).astype(BF16)
        psg = send(ps_s.at[hp], ps_r.at[hp], s_gr.at[4 + hp], r_gr.at[4 + hp], (behind, x))
        sent.append((ppg, spg, dqf, psg))
    for hp in (0, 1):
        grads(0, 0, OWN, hp)

    acc = nn(cx[x], wout[pl.ds(pl.multiple_of(x * width, width), width), :])
    for d, copy in zip((2, 1, 3), cx_sends):
        copy.wait_recv()
        src = lax.rem(x + nx - d, nx)
        acc = acc + nn(cx[src], wout[pl.ds(pl.multiple_of(src * width, width), width), :])
    att_out[...] = acc.astype(BF16)

    for hp in (0, 1):
        ppg, spg, dqf, psg = sent[hp]
        spg.wait_recv()
        psg.wait_recv()
        dqf.wait_recv()
        dkv[OWN, hp] = dkv[OWN, hp] + ps_r[hp].astype(F32) + sp_r[hp].astype(F32)
    dqt[0] = dqt[0] + dqf_r[...].astype(F32)
    g_sends = []
    for d in (2, 1, 3, 0):
        p = lax.rem(x + d, nx)
        at = pl.ds(pl.multiple_of(p * rows, rows), rows)
        parts = [(dqt[0, :, at] * scale).T.astype(BF16)]
        parts += [(dkv[OWN, hp, at, 0:128] * scale).astype(BF16) for hp in (0, 1)]
        parts += [dkv[OWN, hp, at, 128:256].astype(BF16) for hp in (0, 1)]
        column = 0
        for part in parts:
            gs[d, :, column : column + part.shape[1]] = part
            column += part.shape[1]
        if d:
            g_sends.append((d, send(gs.at[d], g.at[d], s_g.at[d], r_g.at[d], (c, p))))

    acc = None
    for d, copy in [(0, None)] + g_sends:
        if copy is not None:
            copy.wait_recv()
        src = lax.rem(x + nx - d, nx)
        cols = pl.ds(pl.multiple_of(src * width, width), width)
        for i in range(3):
            block = (g if d else gs)[d, :, i * width : (i + 1) * width]
            term = nt(block, w3[i, :, cols])
            acc = term if acc is None else acc + term
    gm[pl.ds(HALO, rows), :] = acc.astype(BF16)
    g_up = send(gm.at[pl.ds(rows, HALO), :], gm.at[pl.ds(0, HALO), :], s_h.at[2], r_h.at[2], (up_c, up_x))
    g_dn = send(gm.at[pl.ds(HALO, HALO), :], gm.at[pl.ds(HALO + rows, HALO), :], s_h.at[3], r_h.at[3], (dn_c, dn_x))
    g_up.wait()
    g_dn.wait()
    ext32[...] = gm[...].astype(F32)
    convolve(ig_out, True)

    for d in range(nx):
        z_sends[d].wait_send()
        sp_sends[d].wait_send()
        pp_sends[d].wait_send()
    for copy in [qf, df, of, tf, st] + cx_sends + [copy for _, copy in g_sends]:
        copy.wait_send()
    for group in sent:
        for copy in group:
            copy.wait_send()


def on_device(tokens, conv_kernel, w_qkv, w_out, lengths, cotangent):
    rows, model = tokens.shape
    vmem = lambda shape, dtype: pltpu.VMEM(shape, dtype)
    dma = lambda count: pltpu.SemaphoreType.DMA((count,))
    scratch = [
        vmem((rows + 2 * HALO, model), BF16),
        vmem((rows + 2 * HALO, model), F32),
        vmem((KS, rows, 128), F32),
        vmem((rows, model), BF16),
        vmem((3, model, model), BF16),
        vmem((model, model), BF16),
        vmem((rows, model), BF16),
        vmem((4, rows, 512), BF16),
        vmem((4, rows, 256), BF16),
        vmem((4, rows, 256), BF16),
        vmem((4, 512, 512), BF16),
        vmem((2, 512, 256), BF16),
        vmem((2, 512, 256), BF16),
        vmem((4, 256, 512), BF16),
        vmem((4, 256, 512), BF16),
        vmem((2, 4, 512, 128), BF16),
        vmem((2, 4, 512, 128), BF16),
        vmem((2, 8, 512), I32),
        vmem((5, 4, 512, 512), F32),
        vmem((2, 256, 512), F32),
        vmem((2, 4, 1, 512), F32),
        vmem((256, 512), BF16),
        vmem((256, 512), BF16),
        vmem((8, 512), F32),
        vmem((8, 512), F32),
        vmem((2, 8, 512), F32),
        vmem((8, 512), F32),
        vmem((256, 512), F32),
        vmem((4, rows, 256), BF16),
        vmem((4, rows, 256), BF16),
        vmem((4, 2, 512, 256), F32),
        vmem((2, 256, 512), F32),
        vmem((2, 512, 256), BF16),
        vmem((2, 512, 256), BF16),
        vmem((2, 512, 256), BF16),
        vmem((2, 512, 256), BF16),
        vmem((2, 512, 256), BF16),
        vmem((2, 512, 256), BF16),
        vmem((256, 512), BF16),
        vmem((256, 512), BF16),
        vmem((4, rows, 768), BF16),
        vmem((4, rows, 768), BF16),
        vmem((rows + 2 * HALO, model), BF16),
        dma(6),
    ]
    for count in (4, 4, 4, 4, 4, 4, 4, 5, 4, 8, 4):
        scratch += [dma(count), dma(count)]
    whole = pl.BlockSpec(memory_space=pltpu.VMEM)
    anywhere = pl.BlockSpec(memory_space=pl.ANY)
    out = jax.ShapeDtypeStruct((rows, model), BF16)
    return pl.pallas_call(
        functools.partial(layer_kernel, lax.axis_size("ctx")),
        out_shape=(out, out),
        in_specs=[anywhere, anywhere, anywhere, anywhere, whole, pl.BlockSpec(memory_space=pltpu.SMEM)],
        out_specs=(whole, whole),
        scratch_shapes=scratch,
        compiler_params=pltpu.CompilerParams(
            collective_id=0, has_side_effects=True, vmem_limit_bytes=66_000_000
        ),
    )(tokens, cotangent, w_qkv, w_out, conv_kernel, lengths)


def solution(mesh):
    placed = (P(("ctx", "head"), None), P(), P(), P(), P(), P(("ctx", "head"), None))
    return jax.shard_map(
        on_device,
        mesh=mesh,
        in_specs=placed,
        out_specs=(P(("ctx", "head"), None), P(("ctx", "head"), None)),
        check_vma=False,
    )
```

profile of v0, /device:TPU:1, one launch (start us, length us, event | category | flops | bytes accessed | tf_op | source)
XLA Modules:
  0.0 96.3 jit_solution(14270901404167218523)
XLA Ops:
  0.6 92.3 %shard_map.77 = (bf16[128,1024]{1,0:T(8,128)(2,1)}, bf16[128,1024]{1,0:T(8,128)(2,1)}) custom-call(bf16[128,1024]{1,0:T(8,128)(2,1)} %tok_hbm.1, bf16[128,1024]{1,0:T(8,128)(2,1)} %cot_hbm.1, bf16[1024,3072]{1,0:T(8,128)(2,1)} %wqkv_hbm.1, bf16[1024,1024]{1,0:T(8,128)(2,1)} %wout_hbm.1, f32[7,1024]{1,0:T(8,128)} %convk.1, s32[32]{0:T(128)} %lens.1), custom_call_target="tpu_custom_call" | custom-call | tf_op jit(solution)/shard_map/pallas_call | solution.py:533
  93.0 1.7 %copy.10 = bf16[128,1024]{1,0:T(8,128)(2,1)} copy(bf16[128,1024]{1,0:T(8,128)(2,1)} %get-tuple-element.4) | data formatting | bytes 524288
  94.7 1.7 %copy.11 = bf16[128,1024]{1,0:T(8,128)(2,1)} copy(bf16[128,1024]{1,0:T(8,128)(2,1)} %get-tuple-element.5) | data formatting | bytes 524288
where the time goes:
time: 96.5 us; the launch traced here: 96.3 us
  Pallas kernels  92.3 us (96%)
  local copies, waits for them, and re-layouts  3.34 us (3%)
    pallas_call x1, Pallas kernels, on_device(): pl.pallas_call(functools.partial(layer_kernel, lax.axis_size('ctx')), out...  92.3 us
    unnamed x2, local copies, waits for them, and re-layouts  3.34 us

commit v1 on v0

v1 whole, which is shorter than its diff:
```python
import functools
import math

import jax
import jax.numpy as jnp
from jax import lax
from jax.experimental import pallas as pl
from jax.experimental.pallas import tpu as pltpu
from jax.sharding import PartitionSpec as P

HD = 64
KS = 7
HALO = 16
OWN, PREV, PREVX, PAIR = 0, 1, 2, 3
MESH = pl.DeviceIdType.MESH
F32, BF16, I32 = jnp.float32, jnp.bfloat16, jnp.int32


def nt(a, b):
    return lax.dot_general(a, b, (((1,), (1,)), ((), ())), preferred_element_type=F32)


def nn(a, b):
    return jnp.dot(a, b, preferred_element_type=F32)


def layer_kernel(
    n_ctx,
    tok_hbm,
    cot_hbm,
    wqkv_hbm,
    wout_hbm,
    convk,
    lens,
    att_out,
    ig_out,
    ext,
    ext32,
    cmask,
    cot,
    w3,
    wout,
    mixed,
    kvs,
    qs,
    ds_,
    kv,
    q,
    do,
    kt,
    vt,
    qm,
    dm,
    starts,
    e_ref,
    ot,
    tot,
    of_s,
    of_r,
    tf_s,
    tf_r,
    stat,
    st_s,
    ctxt,
    cxs,
    cx,
    dkv,
    dqt,
    pp_s,
    pp_r,
    sp_s,
    sp_r,
    ps_s,
    ps_r,
    dqf_s,
    dqf_r,
    gs,
    g,
    gm,
    gacc,
    ld,
    s_h,
    r_h,
    s_kv,
    r_kv,
    s_z,
    r_z,
    s_sp,
    r_sp,
    s_pp,
    r_pp,
    s_q,
    r_q,
    s_d,
    r_d,
    s_f,
    r_f,
    s_cx,
    r_cx,
    s_gr,
    r_gr,
    s_g,
    r_g,
):
    c, x = lax.axis_index("ctx"), lax.axis_index("head")
    core = lax.rem(c, 2)
    ahead = lax.rem(c + 2, n_ctx)
    behind = lax.rem(c + n_ctx - 2, n_ctx)
    pair = c + 1 - 2 * core
    rows, width = 128, 256
    seq = 512
    nx = 4
    model = 1024

    up_x = lax.rem(x + 1, nx)
    up_c = lax.rem(c + (x + 1) // nx, n_ctx)
    dn_x = lax.rem(x + nx - 1, nx)
    dn_c = lax.rem(c + n_ctx - (nx - x) // nx, n_ctx)

    loads = [
        pltpu.make_async_copy(tok_hbm, ext.at[pl.ds(HALO, rows), :], ld.at[0]),
        pltpu.make_async_copy(cot_hbm, cot, ld.at[1]),
        pltpu.make_async_copy(wout_hbm, wout, ld.at[2]),
        pltpu.make_async_copy(wqkv_hbm.at[:, pl.ds(model, model)], w3.at[1], ld.at[3]),
        pltpu.make_async_copy(wqkv_hbm.at[:, pl.ds(2 * model, model)], w3.at[2], ld.at[4]),
        pltpu.make_async_copy(wqkv_hbm.at[:, pl.ds(0, model)], w3.at[0], ld.at[5]),
    ]
    for i in (0, 1, 2, 3, 4, 5):
        loads[i].start()

    barrier = pltpu.get_barrier_semaphore()
    peers = [(c, lax.rem(x + d, nx)) for d in (1, 2, 3)]
    peers += [(ahead, x), (behind, x), (pair, x), (up_c, up_x), (dn_c, dn_x)]
    for peer in peers:
        pl.semaphore_signal(barrier, inc=1, device_id=peer, device_id_type=MESH)

    ends = []
    run = jnp.int32(0)
    for i in range(lens.shape[0]):
        run = run + lens[i]
        ends.append(run)
    lane = lax.broadcasted_iota(I32, (8, seq), 1)
    for qi, shard in ((0, c), (1, ahead)):
        pos = shard * seq + lane
        first = jnp.zeros((8, seq), I32)
        for end in ends:
            first = jnp.where(pos >= end, end, first)
        starts[qi] = first
    row_pos = (c * nx + x) * rows + lax.broadcasted_iota(I32, (rows, 128), 0)
    first = jnp.zeros((rows, 128), I32)
    for end in ends:
        first = jnp.where(row_pos >= end, end, first)
    last = jnp.zeros((rows, 128), I32)
    for end in reversed(ends):
        last = jnp.where(row_pos < end, end, last)
    for t in range(KS):
        near = row_pos + (t - KS // 2)
        cmask[t] = jnp.where((near >= first) & (near < last), 1.0, 0.0).astype(F32)
    ot[...] = jnp.zeros_like(ot)
    tot[...] = jnp.zeros_like(tot)
    dqt[...] = jnp.zeros_like(dqt)
    dkv[...] = jnp.zeros_like(dkv)

    def columns(p):
        return pl.ds(pl.multiple_of(p * width, width), width)

    def row_block(p):
        return pl.ds(pl.multiple_of(p * rows, rows), rows)

    peer_at = [lax.rem(x + d, nx) for d in range(nx)]
    source = [lax.rem(x + nx - d, nx) for d in range(nx)]
    mine = row_block(x)

    loads[1].wait()
    loads[2].wait()
    for d in (2, 1, 3, 0):
        block = nt(cot[...], wout[columns(peer_at[d]), :]).astype(BF16)
        if d:
            ds_[d] = block
        else:
            do[0, mine, :] = block
    loads[0].wait()
    pl.semaphore_wait(barrier, len(peers))

    started = []

    def send(src, dst, ss, rs, peer):
        copy = pltpu.make_async_remote_copy(
            src_ref=src, dst_ref=dst, send_sem=ss, recv_sem=rs, device_id=peer, device_id_type=MESH
        )
        copy.start()
        started.append(copy)
        return copy

    def exchange_edges(buf, base):
        up = send(
            buf.at[pl.ds(rows, HALO), :], buf.at[pl.ds(0, HALO), :],
            s_h.at[base], r_h.at[base], (up_c, up_x),
        )
        down = send(
            buf.at[pl.ds(HALO, HALO), :], buf.at[pl.ds(HALO + rows, HALO), :],
            s_h.at[base + 1], r_h.at[base + 1], (dn_c, dn_x),
        )
        return up, down

    def convolve(buf, edges, out, flip):
        def part(at, count):
            def chunk(i, carry):
                lanes = pl.ds(pl.multiple_of(i * 128, 128), 128)
                acc = ext32[pl.ds(HALO + at, count), lanes]
                for t in range(KS):
                    tap = convk[pl.ds(KS - 1 - t if flip else t, 1), lanes]
                    near = ext32[pl.ds(HALO + at - KS // 2 + t, count), lanes]
                    acc = acc + tap * near * cmask[t, pl.ds(at, count), :]
                out[pl.ds(at, count), lanes] = acc.astype(BF16)
                return carry

            lax.fori_loop(0, model // 128, chunk, 0)

        inner = pl.ds(HALO, rows)
        ext32[inner, :] = buf[inner, :].astype(F32)
        part(HALO, rows - 2 * HALO)
        for edge in edges:
            edge.wait_recv()
        for side in (0, HALO + rows):
            ext32[pl.ds(side, HALO), :] = buf[pl.ds(side, HALO), :].astype(F32)
        part(0, HALO)
        part(rows - HALO, HALO)

    edges = exchange_edges(ext, 0)
    d_sends = [
        send(ds_.at[d], do.at[0, mine, :], s_d.at[d], r_d.at[d], (c, peer_at[d])) for d in (2, 1, 3)
    ]
    convolve(ext, edges, mixed, False)

    loads[3].wait()
    loads[4].wait()
    kv_sends = {}
    for d in (2, 1, 3, 0):
        cols = columns(peer_at[d])
        for part in (0, 1):
            block = nn(mixed[...], w3[1 + part, :, cols]).astype(BF16)
            lanes = slice(part * width, (part + 1) * width)
            if d:
                kvs[d, :, lanes] = block
            else:
                kv[OWN, mine, lanes] = block
        if d:
            kv_sends[d] = send(kvs.at[d], kv.at[OWN, mine, :], s_kv.at[d], r_kv.at[d], (c, peer_at[d]))

    z_sends, sp_sends, pp_sends = {}, {}, {}

    def forward(d):
        at = row_block(source[d])
        z_sends[d] = send(kv.at[OWN, at, :], kv.at[PREV, at, :], s_z.at[d], r_z.at[d], (ahead, x))
        sp_sends[d] = send(kv.at[OWN, at, :], kv.at[PAIR, at, :], s_sp.at[d], r_sp.at[d], (pair, x))

    forward(0)

    loads[5].wait()
    q_sends = []
    for d in (2, 1, 3, 0):
        block = nn(mixed[...], w3[0, :, columns(peer_at[d])]).astype(BF16)
        if d:
            qs[d] = block
            q_sends.append(send(qs.at[d], q.at[0, mine, :], s_q.at[d], r_q.at[d], (c, peer_at[d])))
        else:
            q[0, mine, :] = block

    for d in (1, 3, 2):
        kv_sends[d].wait_recv()
        forward(d)
    for copy in q_sends:
        copy.wait_recv()
    qf = send(q.at[0], q.at[1], s_f.at[0], r_f.at[0], (behind, x))
    for copy in d_sends:
        copy.wait_recv()
    df = send(do.at[0], do.at[1], s_f.at[1], r_f.at[1], (behind, x))

    half = lax.broadcasted_iota(I32, (seq, 128), 1) // HD

    def split_heads(src, dst, qi):
        for h in range(4):
            block = src[qi, :, (h // 2) * 128 : (h // 2) * 128 + 128].astype(F32)
            dst[qi, h] = jnp.where(half == h % 2, block, 0.0).astype(BF16)

    def turn(slot):
        kt[slot] = kv[slot, :, 0:width].astype(F32).T.astype(BF16)
        vt[slot] = kv[slot, :, width : 2 * width].astype(F32).T.astype(BF16)

    scale = HD ** -0.5
    scale2 = scale * math.log2(math.e)
    kc = 256
    FULL = ((0, 0, seq), (kc, 0, seq))
    LOWER = ((0, 0, seq), (kc, kc, seq - kc))
    UPPER = ((0, 0, kc), (kc, 0, seq))

    def attend(block, qi, slot, distance, parts):
        base = (jnp.where(qi == 0, c, ahead) - distance) * seq

        def tile(hp, k0, q0, queries):
            lanes = pl.ds(pl.multiple_of(hp * 128, 128), 128)
            at = pl.ds(q0, queries)
            keys = kv[slot, pl.ds(k0, kc), lanes]
            k_iota = lax.broadcasted_iota(I32, (kc, queries), 0)
            ok = base + k0 + k_iota >= starts[qi, 0:1, at]
            if parts is LOWER:
                q_iota = lax.broadcasted_iota(I32, (kc, queries), 1)
                ok = ok & (k0 + k_iota <= q0 + q_iota)
            for s in (0, 1):
                h = hp * 2 + s
                score = nt(keys, qm[qi, h, at, :])
                e = jnp.where(ok, jnp.exp2(score * scale2), 0.0)
                e_ref[block, h, pl.ds(k0, kc), at] = e
                tot[qi, h, :, at] += jnp.sum(e, axis=0, keepdims=True)
                head_rows = pl.ds(pl.multiple_of(h * HD, HD), HD)
                ot[qi, head_rows, at] += nn(vt[slot, head_rows, pl.ds(k0, kc)], e.astype(BF16))

        if parts is FULL:

            def step(i, carry):
                tile(i // 2, pl.multiple_of(lax.rem(i, 2) * kc, kc), 0, seq)
                return carry

            lax.fori_loop(0, 4, step, 0)
        else:

            def step(hp, carry):
                for part in parts:
                    tile(hp, *part)
                return carry

            lax.fori_loop(0, 2, step, 0)

    def grads(block, qi, slot, hp, parts):
        def tile(k0, q0, queries):
            at = pl.ds(q0, queries)
            keys_at = pl.ds(k0, kc)
            values = kv[slot, keys_at, pl.ds(width + hp * 128, 128)]
            for s in (0, 1):
                h = hp * 2 + s
                prob = e_ref[block, h, keys_at, at] * stat[qi, h : h + 1, at]
                d_prob = nt(values, dm[qi, h, at, :])
                d_score = (prob * (d_prob - stat[qi, 4 + h : 5 + h, at])).astype(BF16)
                dkv[slot, hp, keys_at, 128:256] += nn(prob.astype(BF16), dm[qi, h, at, :])
                dkv[slot, hp, keys_at, 0:128] += nn(d_score, qm[qi, h, at, :])
                head_rows = pl.ds(h * HD, HD)
                dqt[qi, head_rows, at] += nn(kt[slot, head_rows, keys_at], d_score)

        if parts is FULL:

            def step(part, carry):
                tile(pl.multiple_of(part * kc, kc), 0, seq)
                return carry

            lax.fori_loop(0, seq // kc, step, 0)
        else:
            for part in parts:
                tile(*part)

    far = 1 - core
    split_heads(q, qm, 0)
    turn(OWN)
    attend(0, 0, OWN, 0, LOWER)
    for d in (0, 1, 3, 2):
        z_sends[d].wait_recv()
        at = row_block(source[d])
        pp_sends[d] = send(kv.at[PREV, at, :], kv.at[PREVX, at, :], s_pp.at[d], r_pp.at[d], (pair, x))
    qf.wait_recv()
    split_heads(q, qm, 1)
    turn(PREV)
    attend(2, 1, PREV, 4, UPPER)
    for d in range(nx):
        pp_sends[d].wait_recv()
        sp_sends[d].wait_recv()
    turn(PREVX)
    turn(PAIR)
    attend(4, far, PREVX + core, 3 - 2 * core, FULL)
    of_s[...] = ot[1].astype(BF16)
    for h in range(4):
        tf_s[h : h + 1, :] = tot[1, h]
        tf_s[4 + h : 5 + h, :] = tot[1, h]
    tf = send(tf_s, tf_r, s_f.at[3], r_f.at[3], (ahead, x))
    of = send(of_s, of_r, s_f.at[2], r_f.at[2], (ahead, x))

    def near_blocks(j, carry):
        attend(1 + 2 * j, 0, PREV + j, 2 - j * (1 - 2 * core), FULL)
        return carry

    lax.fori_loop(0, 2, near_blocks, 0)
    df.wait_recv()
    split_heads(do, dm, 0)
    split_heads(do, dm, 1)
    d_turned = do[0].astype(F32).T
    tf.wait_recv()
    of.wait_recv()

    for h in range(4):
        head_rows = slice(h * HD, (h + 1) * HD)
        total = tot[0, h] + tf_r[h : h + 1, :]
        context = ((ot[0, head_rows, :] + of_r[head_rows, :].astype(F32)) / total).astype(BF16)
        context = context.astype(F32)
        ctxt[head_rows, :] = context
        stat[0, h : h + 1, :] = 1.0 / total
        stat[0, 4 + h : 5 + h, :] = jnp.sum(d_turned[head_rows, :] * context, axis=0, keepdims=True)
    st_s[...] = stat[0]
    st = send(st_s, stat.at[1], s_f.at[4], r_f.at[4], (behind, x))
    cx_sends = {}
    for d in (2, 1, 3, 0):
        block = ctxt[:, row_block(peer_at[d])].T.astype(BF16)
        if d:
            cxs[d] = block
            cx_sends[d] = send(cxs.at[d], cx.at[d], s_cx.at[d], r_cx.at[d], (c, peer_at[d]))
        else:
            cx[0] = block

    sent = []
    for hp in (0, 1):

        def near_grads(j, carry):
            grads(1 + 2 * j, 0, PREV + j, hp, FULL)
            return carry

        lax.fori_loop(0, 2, near_grads, 0)
        if hp == 0:
            st.wait_recv()
        grads(4, far, PREVX + core, hp, FULL)
        pp_s[hp] = dkv[PREVX, hp].astype(BF16)
        ppg = send(pp_s.at[hp], pp_r.at[hp], s_gr.at[hp], r_gr.at[hp], (pair, x))
        sp_s[hp] = dkv[PAIR, hp].astype(BF16)
        spg = send(sp_s.at[hp], sp_r.at[hp], s_gr.at[2 + hp], r_gr.at[2 + hp], (pair, x))
        grads(2, 1, PREV, hp, UPPER)
        dq_rows = pl.ds(hp * 128, 128)
        dqf_s[dq_rows, :] = dqt[1, dq_rows, :].astype(BF16)
        dqf = send(dqf_s.at[dq_rows, :], dqf_r.at[dq_rows, :], s_gr.at[6 + hp], r_gr.at[6 + hp], (ahead, x))
        ppg.wait_recv()
        ps_s[hp] = (dkv[PREV, hp] + pp_r[hp].astype(F32)).astype(BF16)
        psg = send(ps_s.at[hp], ps_r.at[hp], s_gr.at[4 + hp], r_gr.at[4 + hp], (behind, x))
        sent.append((spg, dqf, psg))
    for hp in (0, 1):
        grads(0, 0, OWN, hp, LOWER)

    g_sends = {}

    def give(group):
        if group == 1:
            for _, dqf, _ in sent:
                dqf.wait_recv()
            dqt[0] = (dqt[0] + dqf_r[...].astype(F32)) * scale
        else:
            hp = group // 2
            spg, _, psg = sent[hp]
            spg.wait_recv()
            psg.wait_recv()
        for d in (2, 1, 3, 0):
            at = row_block(peer_at[d])
            out = gs.at[group, d] if d else g.at[group, 0]
            if group == 1:
                out[...] = dqt[0, :, at].T.astype(BF16)
            else:
                hp = group // 2
                total = dkv[OWN, hp, at, :] + ps_r[hp, at, :].astype(F32) + sp_r[hp, at, :].astype(F32)
                out[:, 0:128] = (total[:, 0:128] * scale).astype(BF16)
                out[:, 128:256] = total[:, 128:256].astype(BF16)
            if d:
                slot = group * nx + d
                g_sends[group, d] = send(
                    gs.at[group, d], g.at[group, d], s_g.at[slot], r_g.at[slot], (c, peer_at[d])
                )

    def take(group, d):
        if d:
            g_sends[group, d].wait_recv()
        if group == 1:
            return nt(g[1, d], w3[0, :, columns(source[d])])
        cols = pl.ds(pl.multiple_of(source[d] * width + (group // 2) * 128, 128), 128)
        return nt(g[group, d, :, 0:128], w3[1, :, cols]) + nt(g[group, d, :, 128:256], w3[2, :, cols])

    give(0)
    acc = nn(cx[0], wout[columns(x), :])
    for d in (1, 3, 2):
        cx_sends[d].wait_recv()
        acc = acc + nn(cx[d], wout[columns(source[d]), :])
    att_out[...] = acc.astype(BF16)
    give(1)
    gacc[...] = take(0, 0) + take(1, 0)
    for d in (1, 3, 2):
        gacc[...] += take(0, d)
    give(2)
    for d in (1, 3, 2):
        gacc[...] += take(1, d)
    gacc[...] += take(2, 0)
    for d in (1, 3, 2):
        gacc[...] += take(2, d)
    gm[pl.ds(HALO, rows), :] = gacc[...].astype(BF16)
    convolve(gm, exchange_edges(gm, 2), ig_out, True)

    for copy in started:
        copy.wait_send()


def on_device(tokens, conv_kernel, w_qkv, w_out, lengths, cotangent):
    rows, model = tokens.shape
    vmem = lambda shape, dtype: pltpu.VMEM(shape, dtype)
    dma = lambda count: pltpu.SemaphoreType.DMA((count,))
    scratch = [
        vmem((rows + 2 * HALO, model), BF16),
        vmem((rows + 2 * HALO, model), F32),
        vmem((KS, rows, 128), F32),
        vmem((rows, model), BF16),
        vmem((3, model, model), BF16),
        vmem((model, model), BF16),
        vmem((rows, model), BF16),
        vmem((4, rows, 512), BF16),
        vmem((4, rows, 256), BF16),
        vmem((4, rows, 256), BF16),
        vmem((4, 512, 512), BF16),
        vmem((2, 512, 256), BF16),
        vmem((2, 512, 256), BF16),
        vmem((4, 256, 512), BF16),
        vmem((4, 256, 512), BF16),
        vmem((2, 4, 512, 128), BF16),
        vmem((2, 4, 512, 128), BF16),
        vmem((2, 8, 512), I32),
        vmem((5, 4, 512, 512), F32),
        vmem((2, 256, 512), F32),
        vmem((2, 4, 1, 512), F32),
        vmem((256, 512), BF16),
        vmem((256, 512), BF16),
        vmem((8, 512), F32),
        vmem((8, 512), F32),
        vmem((2, 8, 512), F32),
        vmem((8, 512), F32),
        vmem((256, 512), F32),
        vmem((4, rows, 256), BF16),
        vmem((4, rows, 256), BF16),
        vmem((4, 2, 512, 256), F32),
        vmem((2, 256, 512), F32),
        vmem((2, 512, 256), BF16),
        vmem((2, 512, 256), BF16),
        vmem((2, 512, 256), BF16),
        vmem((2, 512, 256), BF16),
        vmem((2, 512, 256), BF16),
        vmem((2, 512, 256), BF16),
        vmem((256, 512), BF16),
        vmem((256, 512), BF16),
        vmem((3, 4, rows, 256), BF16),
        vmem((3, 4, rows, 256), BF16),
        vmem((rows + 2 * HALO, model), BF16),
        vmem((rows, model), F32),
        dma(6),
    ]
    for count in (4, 4, 4, 4, 4, 4, 4, 5, 4, 8, 12):
        scratch += [dma(count), dma(count)]
    whole = pl.BlockSpec(memory_space=pltpu.VMEM)
    anywhere = pl.BlockSpec(memory_space=pl.ANY)
    out = jax.ShapeDtypeStruct((rows, model), BF16)
    return pl.pallas_call(
        functools.partial(layer_kernel, lax.axis_size("ctx")),
        out_shape=(out, out),
        in_specs=[anywhere, anywhere, anywhere, anywhere, whole, pl.BlockSpec(memory_space=pltpu.SMEM)],
        out_specs=(whole, whole),
        scratch_shapes=scratch,
        compiler_params=pltpu.CompilerParams(
            collective_id=0, has_side_effects=True, vmem_limit_bytes=66_000_000
        ),
    )(tokens, cotangent, w_qkv, w_out, conv_kernel, lengths)


def solution(mesh):
    placed = (P(("ctx", "head"), None), P(), P(), P(), P(), P(("ctx", "head"), None))
    return jax.shard_map(
        on_device,
        mesh=mesh,
        in_specs=placed,
        out_specs=(P(("ctx", "head"), None), P(("ctx", "head"), None)),
        check_vma=False,
    )
```

time: 96.5 us -> 87.2 us (0.904)
  Pallas kernels: 92.3 us -> 83 us
    pallas_call x1, Pallas kernels: 92.3 us -> 83 us  [on_device(): pl.pallas_call(functools.partial(layer_kernel, lax.axis_size('ctx')), out...]
where the time goes in v1:
time: 87.2 us; the launch traced here: 86.9 us
  Pallas kernels  83 us (95%)
  local copies, waits for them, and re-layouts  3.34 us (4%)
    pallas_call x1, Pallas kernels, on_device(): pl.pallas_call(functools.partial(layer_kernel, lax.axis_size('ctx')), out...  83 us
    unnamed x2, local copies, waits for them, and re-layouts  3.34 us

profile of v1, /device:TPU:1, one launch (start us, length us, event | category | flops | bytes accessed | tf_op | source)
XLA Modules:
  0.0 86.9 jit_solution(7787938717829709036)
XLA Ops:
  0.6 83.0 %shard_map.77 = (bf16[128,1024]{1,0:T(8,128)(2,1)}, bf16[128,1024]{1,0:T(8,128)(2,1)}) custom-call(bf16[128,1024]{1,0:T(8,128)(2,1)} %tok_hbm.1, bf16[128,1024]{1,0:T(8,128)(2,1)} %cot_hbm.1, bf16[1024,3072]{1,0:T(8,128)(2,1)} %wqkv_hbm.1, bf16[1024,1024]{1,0:T(8,128)(2,1)} %wout_hbm.1, f32[7,1024]{1,0:T(8,128)} %convk.1, s32[32]{0:T(128)} %lens.1), custom_call_target="tpu_custom_call" | custom-call | tf_op jit(solution)/shard_map/pallas_call | solution.py:558
  83.6 1.7 %copy.10 = bf16[128,1024]{1,0:T(8,128)(2,1)} copy(bf16[128,1024]{1,0:T(8,128)(2,1)} %get-tuple-element.4) | data formatting | bytes 524288
  85.3 1.7 %copy.11 = bf16[128,1024]{1,0:T(8,128)(2,1)} copy(bf16[128,1024]{1,0:T(8,128)(2,1)} %get-tuple-element.5) | data formatting | bytes 524288

commit v2 on v1

v2 whole, which is shorter than its diff:
```python
import functools
import math

import jax
import jax.numpy as jnp
from jax import lax
from jax.experimental import pallas as pl
from jax.experimental.pallas import tpu as pltpu
from jax.sharding import PartitionSpec as P

HD = 64
KS = 7
HALO = 16
OWN, PREV, PREVX, PAIR = 0, 1, 2, 3
MESH = pl.DeviceIdType.MESH
F32, BF16, I32 = jnp.float32, jnp.bfloat16, jnp.int32


def nt(a, b):
    return lax.dot_general(a, b, (((1,), (1,)), ((), ())), preferred_element_type=F32)


def nn(a, b):
    return jnp.dot(a, b, preferred_element_type=F32)


def layer_kernel(
    n_ctx,
    tok_hbm,
    cot_hbm,
    wqkv_hbm,
    wout_hbm,
    convk_hbm,
    lens_hbm,
    att_out,
    ig_out,
    ext,
    ext32,
    cmask,
    cot,
    w3,
    wout,
    mixed,
    kvs,
    qs,
    ds_,
    kv,
    q,
    do,
    kt,
    vt,
    qm,
    dm,
    starts,
    e_ref,
    ot,
    tot,
    of_s,
    of_r,
    tf_s,
    tf_r,
    stat,
    st_s,
    ctxt,
    cxs,
    cx,
    dkv,
    dqt,
    pp_s,
    pp_r,
    sp_s,
    sp_r,
    ps_s,
    ps_r,
    dqf_s,
    dqf_r,
    gs,
    g,
    gm,
    gacc,
    convk,
    lens,
    ld,
    s_h,
    r_h,
    s_kv,
    r_kv,
    s_z,
    r_z,
    s_sp,
    r_sp,
    s_pp,
    r_pp,
    s_q,
    r_q,
    s_d,
    r_d,
    s_qf,
    r_qf,
    s_f,
    r_f,
    s_cx,
    r_cx,
    s_gr,
    r_gr,
    s_g,
    r_g,
):
    c, x = lax.axis_index("ctx"), lax.axis_index("head")
    core = lax.rem(c, 2)
    ahead = lax.rem(c + 2, n_ctx)
    behind = lax.rem(c + n_ctx - 2, n_ctx)
    pair = c + 1 - 2 * core
    rows, width = 128, 256
    seq = 512
    nx = 4
    model = 1024

    up_x = lax.rem(x + 1, nx)
    up_c = lax.rem(c + (x + 1) // nx, n_ctx)
    dn_x = lax.rem(x + nx - 1, nx)
    dn_c = lax.rem(c + n_ctx - (nx - x) // nx, n_ctx)

    loads = [
        pltpu.make_async_copy(tok_hbm, ext.at[pl.ds(HALO, rows), :], ld.at[0]),
        pltpu.make_async_copy(lens_hbm, lens, ld.at[1]),
        pltpu.make_async_copy(convk_hbm, convk, ld.at[2]),
        pltpu.make_async_copy(wqkv_hbm.at[:, pl.ds(model, model)], w3.at[1], ld.at[3]),
        pltpu.make_async_copy(wqkv_hbm.at[:, pl.ds(2 * model, model)], w3.at[2], ld.at[4]),
        pltpu.make_async_copy(wqkv_hbm.at[:, pl.ds(0, model)], w3.at[0], ld.at[5]),
        pltpu.make_async_copy(cot_hbm, cot, ld.at[6]),
        pltpu.make_async_copy(wout_hbm, wout, ld.at[7]),
    ]
    barrier = pltpu.get_barrier_semaphore()
    peers = [(c, lax.rem(x + d, nx)) for d in (1, 2, 3)]
    peers += [(ahead, x), (behind, x), (pair, x), (up_c, up_x), (dn_c, dn_x)]
    for peer in peers:
        pl.semaphore_signal(barrier, inc=1, device_id=peer, device_id_type=MESH)
    for load in loads:
        load.start()
    loads[0].wait()
    pl.semaphore_wait(barrier, len(peers))

    started = []

    def send(src, dst, ss, rs, peer):
        copy = pltpu.make_async_remote_copy(
            src_ref=src, dst_ref=dst, send_sem=ss, recv_sem=rs, device_id=peer, device_id_type=MESH
        )
        copy.start()
        started.append(copy)
        return copy

    def exchange_edges(buf, base):
        up = send(
            buf.at[pl.ds(rows, HALO), :], buf.at[pl.ds(0, HALO), :],
            s_h.at[base], r_h.at[base], (up_c, up_x),
        )
        down = send(
            buf.at[pl.ds(HALO, HALO), :], buf.at[pl.ds(HALO + rows, HALO), :],
            s_h.at[base + 1], r_h.at[base + 1], (dn_c, dn_x),
        )
        return up, down

    edges = exchange_edges(ext, 0)

    loads[1].wait()
    ends = []
    run = jnp.int32(0)
    for i in range(lens.shape[0]):
        run = run + lens[i]
        ends.append(run)
    row_pos = (c * nx + x) * rows + lax.broadcasted_iota(I32, (rows, 128), 0)
    first = jnp.zeros((rows, 128), I32)
    for end in ends:
        first = jnp.where(row_pos >= end, end, first)
    last = jnp.zeros((rows, 128), I32)
    for end in reversed(ends):
        last = jnp.where(row_pos < end, end, last)
    for t in range(KS):
        near = row_pos + (t - KS // 2)
        cmask[t] = jnp.where((near >= first) & (near < last), 1.0, 0.0).astype(F32)

    def columns(p):
        return pl.ds(pl.multiple_of(p * width, width), width)

    def row_block(p):
        return pl.ds(pl.multiple_of(p * rows, rows), rows)

    peer_at = [lax.rem(x + d, nx) for d in range(nx)]
    source = [lax.rem(x + nx - d, nx) for d in range(nx)]
    mine = row_block(x)
    ways = (1, 3, 2)

    def convolve(buf, edges, out, flip):
        def part(at, count):
            def chunk(i, carry):
                lanes = pl.ds(pl.multiple_of(i * 128, 128), 128)
                acc = ext32[pl.ds(HALO + at, count), lanes]
                for t in range(KS):
                    tap = convk[pl.ds(KS - 1 - t if flip else t, 1), lanes]
                    near = ext32[pl.ds(HALO + at - KS // 2 + t, count), lanes]
                    acc = acc + tap * near * cmask[t, pl.ds(at, count), :]
                out[pl.ds(at, count), lanes] = acc.astype(BF16)
                return carry

            lax.fori_loop(0, model // 128, chunk, 0)

        inner = pl.ds(HALO, rows)
        ext32[inner, :] = buf[inner, :].astype(F32)
        part(HALO, rows - 2 * HALO)
        for edge in edges:
            edge.wait_recv()
        for side in (0, HALO + rows):
            ext32[pl.ds(side, HALO), :] = buf[pl.ds(side, HALO), :].astype(F32)
        part(0, HALO)
        part(rows - HALO, HALO)

    loads[2].wait()
    convolve(ext, edges, mixed, False)

    kv_sends, z_sends, sp_sends, pp_sends, q_sends, d_sends, qf_sends = {}, {}, {}, {}, {}, {}, {}

    def give_kv(hp, d):
        slot = hp * nx + d
        kv_sends[hp, d] = send(
            kvs.at[d, hp], kv.at[OWN, hp, mine, :], s_kv.at[slot], r_kv.at[slot], (c, peer_at[d])
        )

    def forward(hp, d):
        at, slot = row_block(source[d]), hp * nx + d
        block = kv.at[OWN, hp, at, :]
        z_sends[hp, d] = send(block, kv.at[PREV, hp, at, :], s_z.at[slot], r_z.at[slot], (ahead, x))
        sp_sends[hp, d] = send(block, kv.at[PAIR, hp, at, :], s_sp.at[slot], r_sp.at[slot], (pair, x))

    def forward_pair(hp, d):
        at, slot = row_block(source[d]), hp * nx + d
        pp_sends[hp, d] = send(
            kv.at[PREV, hp, at, :], kv.at[PREVX, hp, at, :], s_pp.at[slot], r_pp.at[slot], (pair, x)
        )

    def forward_q(d):
        at = row_block(source[d])
        qf_sends[d] = send(q.at[0, at, :], q.at[1, at, :], s_qf.at[d], r_qf.at[d], (behind, x))

    loads[3].wait()
    loads[4].wait()
    for d in (2, 1, 3, 0):
        for part in (0, 1):
            block = nn(mixed[...], w3[1 + part, :, columns(peer_at[d])]).astype(BF16)
            for hp in (0, 1):
                piece = block[:, hp * 128 : hp * 128 + 128]
                if d:
                    kvs[d, hp, :, part * 128 : part * 128 + 128] = piece
                else:
                    kv[OWN, hp, mine, part * 128 : part * 128 + 128] = piece
        if d:
            give_kv(0, d)
    forward(0, 0)
    loads[5].wait()
    for d in (2, 1, 3, 0):
        block = nn(mixed[...], w3[0, :, columns(peer_at[d])]).astype(BF16)
        if d:
            qs[d] = block
            q_sends[d] = send(qs.at[d], q.at[0, mine, :], s_q.at[d], r_q.at[d], (c, peer_at[d]))
        else:
            q[0, mine, :] = block
    forward_q(0)
    for d in (2, 1, 3):
        give_kv(1, d)
    for d in ways:
        kv_sends[0, d].wait_recv()
        forward(0, d)
    forward(1, 0)

    loads[6].wait()
    loads[7].wait()
    for d in (2, 1, 3, 0):
        block = nt(cot[...], wout[columns(peer_at[d]), :]).astype(BF16)
        if d:
            ds_[d] = block
            d_sends[d] = send(ds_.at[d], do.at[0, mine, :], s_d.at[d], r_d.at[d], (c, peer_at[d]))
        else:
            do[0, mine, :] = block
    for d in ways:
        q_sends[d].wait_recv()
        forward_q(d)

    lane = lax.broadcasted_iota(I32, (8, seq), 1)
    for qi, shard in ((0, c), (1, ahead)):
        pos = shard * seq + lane
        first = jnp.zeros((8, seq), I32)
        for end in ends:
            first = jnp.where(pos >= end, end, first)
        starts[qi] = first
    half = lax.broadcasted_iota(I32, (seq, 128), 1) // HD

    def split_heads(src, dst, qi):
        for h in range(4):
            block = src[qi, :, (h // 2) * 128 : (h // 2) * 128 + 128].astype(F32)
            dst[qi, h] = jnp.where(half == h % 2, block, 0.0).astype(BF16)

    def turn(slot, hp):
        kt[slot, hp] = kv[slot, hp, :, 0:128].astype(F32).T.astype(BF16)
        vt[slot, hp] = kv[slot, hp, :, 128:256].astype(F32).T.astype(BF16)

    scale = HD ** -0.5
    scale2 = scale * math.log2(math.e)
    kc = 256
    FULL = ((0, 0, seq), (kc, 0, seq))
    LOWER = ((0, 0, seq), (kc, kc, seq - kc))
    UPPER = ((0, 0, kc), (kc, 0, seq))

    def over_parts(parts, tile):
        if parts is FULL:

            def step(part, carry):
                tile(pl.multiple_of(part * kc, kc), 0, seq)
                return carry

            lax.fori_loop(0, seq // kc, step, 0)
        else:
            for part in parts:
                tile(*part)

    def attend(block, qi, slot, distance, parts, hp):
        base = (jnp.where(qi == 0, c, ahead) - distance) * seq

        def tile(k0, q0, queries):
            at = pl.ds(q0, queries)
            keys = kv[slot, hp, pl.ds(k0, kc), 0:128]
            k_iota = lax.broadcasted_iota(I32, (kc, queries), 0)
            ok = base + k0 + k_iota >= starts[qi, 0:1, at]
            if parts is LOWER:
                q_iota = lax.broadcasted_iota(I32, (kc, queries), 1)
                ok = ok & (k0 + k_iota <= q0 + q_iota)
            for s in (0, 1):
                h = hp * 2 + s
                score = nt(keys, qm[qi, h, at, :])
                e = jnp.where(ok, jnp.exp2(score * scale2), 0.0)
                e_ref[block, h, pl.ds(k0, kc), at] = e
                tot[qi, h, :, at] += jnp.sum(e, axis=0, keepdims=True)
                head_rows = pl.ds(s * HD, HD)
                ot[qi, hp, head_rows, at] += nn(vt[slot, hp, head_rows, pl.ds(k0, kc)], e.astype(BF16))

        over_parts(parts, tile)

    def grads(block, qi, slot, hp, parts):
        def tile(k0, q0, queries):
            at = pl.ds(q0, queries)
            keys_at = pl.ds(k0, kc)
            values = kv[slot, hp, keys_at, 128:256]
            for s in (0, 1):
                h = hp * 2 + s
                prob = e_ref[block, h, keys_at, at] * stat[qi, hp, s : s + 1, at]
                d_prob = nt(values, dm[qi, h, at, :])
                d_score = (prob * (d_prob - stat[qi, hp, 4 + s : 5 + s, at])).astype(BF16)
                dkv[slot, hp, keys_at, 128:256] += nn(prob.astype(BF16), dm[qi, h, at, :])
                dkv[slot, hp, keys_at, 0:128] += nn(d_score, qm[qi, h, at, :])
                head_rows = pl.ds(s * HD, HD)
                dqt[qi, hp, head_rows, at] += nn(kt[slot, hp, head_rows, keys_at], d_score)

        over_parts(parts, tile)

    far = 1 - core
    ot[...] = jnp.zeros_like(ot)
    tot[...] = jnp.zeros_like(tot)
    split_heads(q, qm, 0)
    turn(OWN, 0)
    attend(0, 0, OWN, 0, LOWER, 0)
    for d in ways:
        kv_sends[1, d].wait_recv()
        forward(1, d)
    for d in ways:
        d_sends[d].wait_recv()
    df = send(do.at[0], do.at[1], s_f.at[0], r_f.at[0], (behind, x))
    turn(OWN, 1)
    attend(0, 0, OWN, 0, LOWER, 1)
    dqt[...] = jnp.zeros_like(dqt)
    dkv[...] = jnp.zeros_like(dkv)
    for d in range(nx):
        qf_sends[d].wait_recv()
    split_heads(q, qm, 1)
    of_sends = []
    for hp in (0, 1):
        for d in (0, 1, 3, 2):
            z_sends[hp, d].wait_recv()
            forward_pair(hp, d)
        turn(PREV, hp)
        attend(2, 1, PREV, 4, UPPER, hp)
        for d in range(nx):
            pp_sends[hp, d].wait_recv()
            sp_sends[hp, d].wait_recv()
        turn(PREVX, hp)
        turn(PAIR, hp)
        attend(4, far, PREVX + core, 3 - 2 * core, FULL, hp)
        of_s[hp] = ot[1, hp].astype(BF16)
        for s in (0, 1):
            for row in range(4):
                tf_s[hp, row * 2 + s : row * 2 + s + 1, :] = tot[1, hp * 2 + s]
        of_sends.append(
            (
                send(tf_s.at[hp], tf_r.at[hp], s_f.at[1 + hp], r_f.at[1 + hp], (ahead, x)),
                send(of_s.at[hp], of_r.at[hp], s_f.at[3 + hp], r_f.at[3 + hp], (ahead, x)),
            )
        )

        def near_blocks(j, carry):
            attend(1 + 2 * j, 0, PREV + j, 2 - j * (1 - 2 * core), FULL, hp)
            return carry

        lax.fori_loop(0, 2, near_blocks, 0)
    df.wait_recv()
    split_heads(do, dm, 0)
    split_heads(do, dm, 1)

    sent, cx_sends = [], {}
    for hp in (0, 1):
        for copy in of_sends[hp]:
            copy.wait_recv()
        d_turned = do[0, :, hp * 128 : hp * 128 + 128].astype(F32).T
        for s in (0, 1):
            head_rows = slice(s * HD, (s + 1) * HD)
            total = tot[0, hp * 2 + s] + tf_r[hp, s : s + 1, :]
            whole = ot[0, hp, head_rows, :] + of_r[hp, head_rows, :].astype(F32)
            context = (whole / total).astype(BF16).astype(F32)
            ctxt[head_rows, :] = context
            st_s[hp, s : s + 1, :] = 1.0 / total
            st_s[hp, 4 + s : 5 + s, :] = jnp.sum(d_turned[head_rows, :] * context, axis=0, keepdims=True)
        stat[0, hp] = st_s[hp]
        st = send(st_s.at[hp], stat.at[1, hp], s_f.at[5 + hp], r_f.at[5 + hp], (behind, x))
        lanes = pl.ds(hp * 128, 128)
        for d in (2, 1, 3, 0):
            block = ctxt[:, row_block(peer_at[d])].T.astype(BF16)
            if d:
                slot = hp * nx + d
                cxs[hp, d] = block
                cx_sends[hp, d] = send(
                    cxs.at[hp, d], cx.at[d, :, lanes], s_cx.at[slot], r_cx.at[slot], (c, peer_at[d])
                )
            else:
                cx[0, :, lanes] = block

        def near_grads(j, carry):
            grads(1 + 2 * j, 0, PREV + j, hp, FULL)
            return carry

        lax.fori_loop(0, 2, near_grads, 0)
        st.wait_recv()
        grads(4, far, PREVX + core, hp, FULL)
        pp_s[hp] = dkv[PREVX, hp].astype(BF16)
        ppg = send(pp_s.at[hp], pp_r.at[hp], s_gr.at[hp], r_gr.at[hp], (pair, x))
        sp_s[hp] = dkv[PAIR, hp].astype(BF16)
        spg = send(sp_s.at[hp], sp_r.at[hp], s_gr.at[2 + hp], r_gr.at[2 + hp], (pair, x))
        grads(2, 1, PREV, hp, UPPER)
        dqf_s[hp] = dqt[1, hp].astype(BF16)
        dqf = send(dqf_s.at[hp], dqf_r.at[hp], s_gr.at[6 + hp], r_gr.at[6 + hp], (ahead, x))
        ppg.wait_recv()
        ps_s[hp] = (dkv[PREV, hp] + pp_r[hp].astype(F32)).astype(BF16)
        psg = send(ps_s.at[hp], ps_r.at[hp], s_gr.at[4 + hp], r_gr.at[4 + hp], (behind, x))
        sent.append((spg, dqf, psg))
    for hp in (0, 1):
        grads(0, 0, OWN, hp, LOWER)

    g_sends = {}

    def give(group):
        if group == 1:
            for hp in (0, 1):
                sent[hp][1].wait_recv()
                dqt[0, hp] = (dqt[0, hp] + dqf_r[hp].astype(F32)) * scale
        else:
            hp = group // 2
            spg, _, psg = sent[hp]
            spg.wait_recv()
            psg.wait_recv()
        for d in (2, 1, 3, 0):
            at = row_block(peer_at[d])
            out = gs.at[group, d] if d else g.at[group, 0]
            if group == 1:
                for hp in (0, 1):
                    out[:, hp * 128 : hp * 128 + 128] = dqt[0, hp, :, at].T.astype(BF16)
            else:
                hp = group // 2
                total = dkv[OWN, hp, at, :] + ps_r[hp, at, :].astype(F32) + sp_r[hp, at, :].astype(F32)
                out[:, 0:128] = (total[:, 0:128] * scale).astype(BF16)
                out[:, 128:256] = total[:, 128:256].astype(BF16)
            if d:
                slot = group * nx + d
                g_sends[group, d] = send(
                    gs.at[group, d], g.at[group, d], s_g.at[slot], r_g.at[slot], (c, peer_at[d])
                )

    def take(group, d):
        if d:
            g_sends[group, d].wait_recv()
        if group == 1:
            return nt(g[1, d], w3[0, :, columns(source[d])])
        cols = pl.ds(pl.multiple_of(source[d] * width + (group // 2) * 128, 128), 128)
        return nt(g[group, d, :, 0:128], w3[1, :, cols]) + nt(g[group, d, :, 128:256], w3[2, :, cols])

    give(0)
    give(1)
    acc = nn(cx[0], wout[columns(x), :])
    for d in ways:
        for hp in (0, 1):
            cx_sends[hp, d].wait_recv()
        acc = acc + nn(cx[d], wout[columns(source[d]), :])
    att_out[...] = acc.astype(BF16)
    gacc[...] = take(0, 0) + take(1, 0)
    for d in ways:
        gacc[...] += take(0, d)
    give(2)
    for d in ways:
        gacc[...] += take(1, d)
    gacc[...] += take(2, 0)
    for d in ways:
        gacc[...] += take(2, d)
    gm[pl.ds(HALO, rows), :] = gacc[...].astype(BF16)
    convolve(gm, exchange_edges(gm, 2), ig_out, True)

    for copy in started:
        copy.wait_send()


def settle_kernel(a_hbm, b_hbm, a_out, b_out, held, sems):
    ins = [pltpu.make_async_copy(src, held.at[i], sems.at[i]) for i, src in enumerate((a_hbm, b_hbm))]
    outs = [pltpu.make_async_copy(held.at[i], dst, sems.at[2 + i]) for i, dst in enumerate((a_out, b_out))]
    for copy in ins:
        copy.start()
    for first, second in zip(ins, outs):
        first.wait()
        second.start()
    for copy in outs:
        copy.wait()


def on_device(tokens, conv_kernel, w_qkv, w_out, lengths, cotangent):
    rows, model = tokens.shape
    vmem = lambda shape, dtype: pltpu.VMEM(shape, dtype)
    dma = lambda count: pltpu.SemaphoreType.DMA((count,))
    scratch = [
        vmem((rows + 2 * HALO, model), BF16),
        vmem((rows + 2 * HALO, model), F32),
        vmem((KS, rows, 128), F32),
        vmem((rows, model), BF16),
        vmem((3, model, model), BF16),
        vmem((model, model), BF16),
        vmem((rows, model), BF16),
        vmem((4, 2, rows, 256), BF16),
        vmem((4, rows, 256), BF16),
        vmem((4, rows, 256), BF16),
        vmem((4, 2, 512, 256), BF16),
        vmem((2, 512, 256), BF16),
        vmem((2, 512, 256), BF16),
        vmem((4, 2, 128, 512), BF16),
        vmem((4, 2, 128, 512), BF16),
        vmem((2, 4, 512, 128), BF16),
        vmem((2, 4, 512, 128), BF16),
        vmem((2, 8, 512), I32),
        vmem((5, 4, 512, 512), F32),
        vmem((2, 2, 128, 512), F32),
        vmem((2, 4, 1, 512), F32),
        vmem((2, 128, 512), BF16),
        vmem((2, 128, 512), BF16),
        vmem((2, 8, 512), F32),
        vmem((2, 8, 512), F32),
        vmem((2, 2, 8, 512), F32),
        vmem((2, 8, 512), F32),
        vmem((128, 512), F32),
        vmem((2, 4, rows, 128), BF16),
        vmem((4, rows, 256), BF16),
        vmem((4, 2, 512, 256), F32),
        vmem((2, 2, 128, 512), F32),
        vmem((2, 512, 256), BF16),
        vmem((2, 512, 256), BF16),
        vmem((2, 512, 256), BF16),
        vmem((2, 512, 256), BF16),
        vmem((2, 512, 256), BF16),
        vmem((2, 512, 256), BF16),
        vmem((2, 128, 512), BF16),
        vmem((2, 128, 512), BF16),
        vmem((3, 4, rows, 256), BF16),
        vmem((3, 4, rows, 256), BF16),
        vmem((rows + 2 * HALO, model), BF16),
        vmem((rows, model), F32),
        vmem(conv_kernel.shape, F32),
        pltpu.SMEM(lengths.shape, I32),
        dma(8),
    ]
    for count in (4, 8, 8, 8, 8, 4, 4, 4, 7, 8, 8, 12):
        scratch += [dma(count), dma(count)]
    whole = pl.BlockSpec(memory_space=pltpu.VMEM)
    anywhere = pl.BlockSpec(memory_space=pl.ANY)
    out = jax.ShapeDtypeStruct((rows, model), BF16)
    attended, input_grad = pl.pallas_call(
        functools.partial(layer_kernel, lax.axis_size("ctx")),
        out_shape=(out, out),
        in_specs=[anywhere] * 6,
        out_specs=(whole, whole),
        scratch_shapes=scratch,
        compiler_params=pltpu.CompilerParams(
            collective_id=0, has_side_effects=True, vmem_limit_bytes=66_000_000
        ),
    )(tokens, cotangent, w_qkv, w_out, conv_kernel, lengths)
    return pl.pallas_call(
        settle_kernel,
        out_shape=(out, out),
        in_specs=[anywhere] * 2,
        out_specs=(anywhere, anywhere),
        scratch_shapes=[vmem((2, rows, model), BF16), dma(4)],
    )(attended, input_grad)


def solution(mesh):
    placed = (P(("ctx", "head"), None), P(), P(), P(), P(), P(("ctx", "head"), None))
    return jax.shard_map(
        on_device,
        mesh=mesh,
        in_specs=placed,
        out_specs=(P(("ctx", "head"), None), P(("ctx", "head"), None)),
        check_vma=False,
    )
```

time: 87.2 us -> 82.1 us (0.942)
  local copies, waits for them, and re-layouts: 3.34 us -> 0 us
  Pallas kernels: 83 us -> 81.2 us
    pallas_call x1, Pallas kernels: 83 us -> 79.4 us  [on_device(): pl.pallas_call(functools.partial(layer_kernel, lax.axis_size('ctx')), out...]
    unnamed x2 -> x0, local copies, waits for them, and re-layouts: 3.34 us -> none
    pallas_call x0 -> x1, Pallas kernels: none -> 1.77 us  [on_device(): pl.pallas_call(settle_kernel, out_shape=(out, out), in_specs=[anywhere] *...]
where the time goes in v2:
time: 82.1 us; the launch traced here: 82 us
  Pallas kernels  81.2 us (99%)
    pallas_call x1, Pallas kernels, on_device(): pl.pallas_call(functools.partial(layer_kernel, lax.axis_size('ctx')), out...  79.4 us
    pallas_call x1, Pallas kernels, on_device(): pl.pallas_call(settle_kernel, out_shape=(out, out), in_specs=[anywhere] *...  1.77 us

profile of v2, /device:TPU:1, one launch (start us, length us, event | category | flops | bytes accessed | tf_op | source)
XLA Modules:
  0.0 82.0 jit_solution(15356331336577608729)
XLA Ops:
  0.6 79.4 %shard_map.77 = (bf16[128,1024]{1,0:T(8,128)(2,1)}, bf16[128,1024]{1,0:T(8,128)(2,1)}) custom-call(bf16[128,1024]{1,0:T(8,128)(2,1)} %tok_hbm.1, bf16[128,1024]{1,0:T(8,128)(2,1)} %cot_hbm.1, bf16[1024,3072]{1,0:T(8,128)(2,1)} %wqkv_hbm.1, bf16[1024,1024]{1,0:T(8,128)(2,1)} %wout_hbm.1, f32[7,1024]{1,0:T(8,128)} %convk_hbm.1, s32[32]{0:T(128)} %lens_hbm.1), custom_call_target="tpu_custom_call" | custom-call | tf_op jit(solution)/shard_map/pallas_call | solution.py:596
  80.0 1.8 %shard_map.78 = (bf16[128,1024]{1,0:T(8,128)(2,1)}, bf16[128,1024]{1,0:T(8,128)(2,1)}) custom-call(bf16[128,1024]{1,0:T(8,128)(2,1)} %get-tuple-element.4.a_hbm, bf16[128,1024]{1,0:T(8,128)(2,1)} %get-tuple-element.5.b_hbm), custom_call_target="tpu_custom_call" | custom-call | tf_op jit(solution)/shard_map/pallas_call | solution.py:606

commit v3 on v2

--- a/solution.py
+++ b/solution.py
@@ -239,9 +239,17 @@
             kv.at[PREV, hp, at, :], kv.at[PREVX, hp, at, :], s_pp.at[slot], r_pp.at[slot], (pair, x)
         )
 
-    def forward_q(d):
-        at = row_block(source[d])
-        qf_sends[d] = send(q.at[0, at, :], q.at[1, at, :], s_qf.at[d], r_qf.at[d], (behind, x))
+    def forward_q(hp, d):
+        at, slot = row_block(source[d]), hp * nx + d
+        qf_sends[hp, d] = send(
+            q.at[0, hp, at, :], q.at[1, hp, at, :], s_qf.at[slot], r_qf.at[slot], (behind, x)
+        )
+
+    def give_q(hp, d):
+        slot = hp * nx + d
+        q_sends[hp, d] = send(
+            qs.at[d, hp], q.at[0, hp, mine, :], s_q.at[slot], r_q.at[slot], (c, peer_at[d])
+        )
 
     loads[3].wait()
     loads[4].wait()
@@ -260,18 +268,24 @@
     loads[5].wait()
     for d in (2, 1, 3, 0):
         block = nn(mixed[...], w3[0, :, columns(peer_at[d])]).astype(BF16)
+        for hp in (0, 1):
+            piece = block[:, hp * 128 : hp * 128 + 128]
+            if d:
+                qs[d, hp] = piece
+            else:
+                q[0, hp, mine, :] = piece
         if d:
-            qs[d] = block
-            q_sends[d] = send(qs.at[d], q.at[0, mine, :], s_q.at[d], r_q.at[d], (c, peer_at[d]))
-        else:
-            q[0, mine, :] = block
-    forward_q(0)
+            give_q(0, d)
+    forward_q(0, 0)
     for d in (2, 1, 3):
         give_kv(1, d)
+    for d in (2, 1, 3):
+        give_q(1, d)
     for d in ways:
         kv_sends[0, d].wait_recv()
         forward(0, d)
     forward(1, 0)
+    forward_q(1, 0)
 
     loads[6].wait()
     loads[7].wait()
@@ -282,9 +296,10 @@
             d_sends[d] = send(ds_.at[d], do.at[0, mine, :], s_d.at[d], r_d.at[d], (c, peer_at[d]))
         else:
             do[0, mine, :] = block
-    for d in ways:
-        q_sends[d].wait_recv()
-        forward_q(d)
+    ot[...] = jnp.zeros_like(ot)
+    tot[...] = jnp.zeros_like(tot)
+    dqt[...] = jnp.zeros_like(dqt)
+    dkv[...] = jnp.zeros_like(dkv)
 
     lane = lax.broadcasted_iota(I32, (8, seq), 1)
     for qi, shard in ((0, c), (1, ahead)):
@@ -294,11 +309,14 @@
             first = jnp.where(pos >= end, end, first)
         starts[qi] = first
     half = lax.broadcasted_iota(I32, (seq, 128), 1) // HD
-
-    def split_heads(src, dst, qi):
-        for h in range(4):
-            block = src[qi, :, (h // 2) * 128 : (h // 2) * 128 + 128].astype(F32)
-            dst[qi, h] = jnp.where(half == h % 2, block, 0.0).astype(BF16)
+    for d in ways:
+        q_sends[0, d].wait_recv()
+        forward_q(0, d)
+
+    def split_pair(block, dst, qi, hp):
+        block = block.astype(F32)
+        for s in (0, 1):
+            dst[qi, hp * 2 + s] = jnp.where(half == s, block, 0.0).astype(BF16)
 
     def turn(slot, hp):
         kt[slot, hp] = kv[slot, hp, :, 0:128].astype(F32).T.astype(BF16)
@@ -345,55 +363,65 @@
 
         over_parts(parts, tile)
 
-    def grads(block, qi, slot, hp, parts):
-        def tile(k0, q0, queries):
-            at = pl.ds(q0, queries)
-            keys_at = pl.ds(k0, kc)
-            values = kv[slot, hp, keys_at, 128:256]
-            for s in (0, 1):
-                h = hp * 2 + s
-                prob = e_ref[block, h, keys_at, at] * stat[qi, hp, s : s + 1, at]
-                d_prob = nt(values, dm[qi, h, at, :])
-                d_score = (prob * (d_prob - stat[qi, hp, 4 + s : 5 + s, at])).astype(BF16)
-                dkv[slot, hp, keys_at, 128:256] += nn(prob.astype(BF16), dm[qi, h, at, :])
-                dkv[slot, hp, keys_at, 0:128] += nn(d_score, qm[qi, h, at, :])
-                head_rows = pl.ds(s * HD, HD)
-                dqt[qi, hp, head_rows, at] += nn(kt[slot, hp, head_rows, keys_at], d_score)
-
-        over_parts(parts, tile)
+    def grads(block, qi, slot, hp, k0, q0, queries):
+        at = pl.ds(q0, queries)
+        keys_at = pl.ds(k0, kc)
+        values = kv[slot, hp, keys_at, 128:256]
+        for s in (0, 1):
+            h = hp * 2 + s
+            prob = e_ref[block, h, keys_at, at] * stat[qi, hp, s : s + 1, at]
+            d_prob = nt(values, dm[qi, h, at, :])
+            d_score = (prob * (d_prob - stat[qi, hp, 4 + s : 5 + s, at])).astype(BF16)
+            dkv[slot, hp, keys_at, 128:256] += nn(prob.astype(BF16), dm[qi, h, at, :])
+            dkv[slot, hp, keys_at, 0:128] += nn(d_score, qm[qi, h, at, :])
+            head_rows = pl.ds(s * HD, HD)
+            dqt[qi, hp, head_rows, at] += nn(kt[slot, hp, head_rows, keys_at], d_score)
 
     far = 1 - core
-    ot[...] = jnp.zeros_like(ot)
-    tot[...] = jnp.zeros_like(tot)
-    split_heads(q, qm, 0)
-    turn(OWN, 0)
-    attend(0, 0, OWN, 0, LOWER, 0)
-    for d in ways:
-        kv_sends[1, d].wait_recv()
-        forward(1, d)
-    for d in ways:
-        d_sends[d].wait_recv()
-    df = send(do.at[0], do.at[1], s_f.at[0], r_f.at[0], (behind, x))
-    turn(OWN, 1)
-    attend(0, 0, OWN, 0, LOWER, 1)
-    dqt[...] = jnp.zeros_like(dqt)
-    dkv[...] = jnp.zeros_like(dkv)
-    for d in range(nx):
-        qf_sends[d].wait_recv()
-    split_heads(q, qm, 1)
-    of_sends = []
-    for hp in (0, 1):
+    def pass_pair(hp):
         for d in (0, 1, 3, 2):
             z_sends[hp, d].wait_recv()
             forward_pair(hp, d)
+
+    def pass_on(d):
+        kv_sends[1, d].wait_recv()
+        forward(1, d)
+        q_sends[1, d].wait_recv()
+        forward_q(1, d)
+
+    of_sends = []
+    for hp in (0, 1):
+        split_pair(q[0, hp], qm, 0, hp)
+        turn(OWN, hp)
+        attend(0, 0, OWN, 0, LOWER, hp)
+        if hp == 1:
+            for d in ways:
+                d_sends[d].wait_recv()
+            df = send(do.at[0], do.at[1], s_f.at[0], r_f.at[0], (behind, x))
+        pass_pair(hp)
+        for d in range(nx):
+            qf_sends[hp, d].wait_recv()
+        split_pair(q[1, hp], qm, 1, hp)
         turn(PREV, hp)
         attend(2, 1, PREV, 4, UPPER, hp)
+        if hp == 0:
+            pass_on(1)
+            pass_on(3)
+        attend(1, 0, PREV, 2, FULL, hp)
+        if hp == 0:
+            pass_on(2)
         for d in range(nx):
             pp_sends[hp, d].wait_recv()
             sp_sends[hp, d].wait_recv()
         turn(PREVX, hp)
         turn(PAIR, hp)
-        attend(4, far, PREVX + core, 3 - 2 * core, FULL, hp)
+
+        def crossed(j, carry):
+            distance = jnp.where(j == 0, 3 - 2 * core, 1 + 2 * core)
+            attend(4 - j, (1 - j) * far, PREVX + (1 - j) * core, distance, FULL, hp)
+            return carry
+
+        lax.fori_loop(0, 2, crossed, 0)
         of_s[hp] = ot[1, hp].astype(BF16)
         for s in (0, 1):
             for row in range(4):
@@ -404,17 +432,56 @@
                 send(of_s.at[hp], of_r.at[hp], s_f.at[3 + hp], r_f.at[3 + hp], (ahead, x)),
             )
         )
-
-        def near_blocks(j, carry):
-            attend(1 + 2 * j, 0, PREV + j, 2 - j * (1 - 2 * core), FULL, hp)
-            return carry
-
-        lax.fori_loop(0, 2, near_blocks, 0)
     df.wait_recv()
-    split_heads(do, dm, 0)
-    split_heads(do, dm, 1)
-
-    sent, cx_sends = [], {}
+    for qi in (0, 1):
+        for hp in (0, 1):
+            split_pair(do[qi, :, hp * 128 : hp * 128 + 128], dm, qi, hp)
+
+    g_sends = {}
+    sent = [[], []]
+    dqf_sends = [None, None]
+    waiting = []
+
+    def pass_back():
+        while waiting:
+            hp, part, ppg = waiting.pop()
+            keys_at = pl.ds(part * kc, kc)
+            slot = 8 + hp * 2 + part
+            ppg.wait_recv()
+            ps_s[hp, keys_at, :] = (dkv[PREV, hp, keys_at, :] + pp_r[hp, keys_at, :].astype(F32)).astype(BF16)
+            sent[hp].append(
+                send(
+                    ps_s.at[hp, keys_at, :], ps_r.at[hp, keys_at, :], s_gr.at[slot], r_gr.at[slot], (behind, x)
+                )
+            )
+
+    def give(group):
+        if group == 1:
+            for hp in (0, 1):
+                dqf_sends[hp].wait_recv()
+                dqt[0, hp] = (dqt[0, hp] + dqf_r[hp].astype(F32)) * scale
+        else:
+            hp = group // 2
+            for copy in sent[hp]:
+                copy.wait_recv()
+        for d in (2, 1, 3, 0):
+            at = row_block(peer_at[d])
+            out = gs.at[group, d] if d else g.at[group, 0]
+            if group == 1:
+                for hp in (0, 1):
+                    out[:, hp * 128 : hp * 128 + 128] = dqt[0, hp, :, at].T.astype(BF16)
+            else:
+                hp = group // 2
+                total = dkv[OWN, hp, at, :] + ps_r[hp, at, :].astype(F32) + sp_r[hp, at, :].astype(F32)
+                out[:, 0:128] = (total[:, 0:128] * scale).astype(BF16)
+                out[:, 128:256] = total[:, 128:256].astype(BF16)
+            if d:
+                slot = group * nx + d
+                g_sends[group, d] = send(
+                    gs.at[group, d], g.at[group, d], s_g.at[slot], r_g.at[slot], (c, peer_at[d])
+                )
+
+    cx_sends = {}
     for hp in (0, 1):
         for copy in of_sends[hp]:
             copy.wait_recv()
@@ -441,55 +508,44 @@
             else:
                 cx[0, :, lanes] = block
 
-        def near_grads(j, carry):
-            grads(1 + 2 * j, 0, PREV + j, hp, FULL)
-            return carry
-
-        lax.fori_loop(0, 2, near_grads, 0)
-        st.wait_recv()
-        grads(4, far, PREVX + core, hp, FULL)
-        pp_s[hp] = dkv[PREVX, hp].astype(BF16)
-        ppg = send(pp_s.at[hp], pp_r.at[hp], s_gr.at[hp], r_gr.at[hp], (pair, x))
-        sp_s[hp] = dkv[PAIR, hp].astype(BF16)
-        spg = send(sp_s.at[hp], sp_r.at[hp], s_gr.at[2 + hp], r_gr.at[2 + hp], (pair, x))
-        grads(2, 1, PREV, hp, UPPER)
-        dqf_s[hp] = dqt[1, hp].astype(BF16)
-        dqf = send(dqf_s.at[hp], dqf_r.at[hp], s_gr.at[6 + hp], r_gr.at[6 + hp], (ahead, x))
-        ppg.wait_recv()
-        ps_s[hp] = (dkv[PREV, hp] + pp_r[hp].astype(F32)).astype(BF16)
-        psg = send(ps_s.at[hp], ps_r.at[hp], s_gr.at[4 + hp], r_gr.at[4 + hp], (behind, x))
-        sent.append((spg, dqf, psg))
-    for hp in (0, 1):
-        grads(0, 0, OWN, hp, LOWER)
-
-    g_sends = {}
-
-    def give(group):
-        if group == 1:
-            for hp in (0, 1):
-                sent[hp][1].wait_recv()
-                dqt[0, hp] = (dqt[0, hp] + dqf_r[hp].astype(F32)) * scale
-        else:
-            hp = group // 2
-            spg, _, psg = sent[hp]
-            spg.wait_recv()
-            psg.wait_recv()
-        for d in (2, 1, 3, 0):
-            at = row_block(peer_at[d])
-            out = gs.at[group, d] if d else g.at[group, 0]
-            if group == 1:
-                for hp in (0, 1):
-                    out[:, hp * 128 : hp * 128 + 128] = dqt[0, hp, :, at].T.astype(BF16)
-            else:
-                hp = group // 2
-                total = dkv[OWN, hp, at, :] + ps_r[hp, at, :].astype(F32) + sp_r[hp, at, :].astype(F32)
-                out[:, 0:128] = (total[:, 0:128] * scale).astype(BF16)
-                out[:, 128:256] = total[:, 128:256].astype(BF16)
-            if d:
-                slot = group * nx + d
-                g_sends[group, d] = send(
-                    gs.at[group, d], g.at[group, d], s_g.at[slot], r_g.at[slot], (c, peer_at[d])
+        for part in (0, 1):
+            k0 = part * kc
+            keys_at = pl.ds(k0, kc)
+            slot = hp * 2 + part
+
+            def near_grads(j, carry):
+                grads(1 + 2 * j, 0, PREV + j, hp, k0, 0, seq)
+                return carry
+
+            lax.fori_loop(0, 2, near_grads, 0)
+            pass_back()
+            if part == 0:
+                st.wait_recv()
+            grads(4, far, PREVX + core, hp, k0, 0, seq)
+            pp_s[hp, keys_at, :] = dkv[PREVX, hp, keys_at, :].astype(BF16)
+            ppg = send(
+                pp_s.at[hp, keys_at, :], pp_r.at[hp, keys_at, :], s_gr.at[slot], r_gr.at[slot], (pair, x)
+            )
+            sp_s[hp, keys_at, :] = dkv[PAIR, hp, keys_at, :].astype(BF16)
+            sent[hp].append(
+                send(
+                    sp_s.at[hp, keys_at, :], sp_r.at[hp, keys_at, :],
+                    s_gr.at[4 + slot], r_gr.at[4 + slot], (pair, x),
                 )
+            )
+            grads(2, 1, PREV, hp, *UPPER[part])
+            waiting.append((hp, part, ppg))
+            if part == 1:
+                dqf_s[hp] = dqt[1, hp].astype(BF16)
+                dqf_sends[hp] = send(
+                    dqf_s.at[hp], dqf_r.at[hp], s_gr.at[12 + hp], r_gr.at[12 + hp], (ahead, x)
+                )
+                if hp == 1:
+                    give(0)
+                grads(0, 0, OWN, hp, *LOWER[1])
+                pass_back()
+                grads(0, 0, OWN, hp, *LOWER[0])
+    give(1)
 
     def take(group, d):
         if d:
@@ -499,8 +555,6 @@
         cols = pl.ds(pl.multiple_of(source[d] * width + (group // 2) * 128, 128), 128)
         return nt(g[group, d, :, 0:128], w3[1, :, cols]) + nt(g[group, d, :, 128:256], w3[2, :, cols])
 
-    give(0)
-    give(1)
     acc = nn(cx[0], wout[columns(x), :])
     for d in ways:
         for hp in (0, 1):
@@ -548,10 +602,10 @@
         vmem((model, model), BF16),
         vmem((rows, model), BF16),
         vmem((4, 2, rows, 256), BF16),
-        vmem((4, rows, 256), BF16),
+        vmem((4, 2, rows, 128), BF16),
         vmem((4, rows, 256), BF16),
         vmem((4, 2, 512, 256), BF16),
-        vmem((2, 512, 256), BF16),
+        vmem((2, 2, 512, 128), BF16),
         vmem((2, 512, 256), BF16),
         vmem((4, 2, 128, 512), BF16),
         vmem((4, 2, 128, 512), BF16),
@@ -588,7 +642,7 @@
         pltpu.SMEM(lengths.shape, I32),
         dma(8),
     ]
-    for count in (4, 8, 8, 8, 8, 4, 4, 4, 7, 8, 8, 12):
+    for count in (4, 8, 8, 8, 8, 8, 4, 8, 7, 8, 14, 12):
         scratch += [dma(count), dma(count)]
     whole = pl.BlockSpec(memory_space=pltpu.VMEM)
     anywhere = pl.BlockSpec(memory_space=pl.ANY)

time: 82.1 us -> 82.7 us (level)
  no operation moved by 1% of the time
where the time goes in v3:
time: 82.7 us; the launch traced here: 82.6 us
  Pallas kernels  81.8 us (99%)
    pallas_call x1, Pallas kernels, on_device(): pl.pallas_call(functools.partial(layer_kernel, lax.axis_size('ctx')), out...  80 us
    pallas_call x1, Pallas kernels, on_device(): pl.pallas_call(settle_kernel, out_shape=(out, out), in_specs=[anywhere] *...  1.77 us

profile of v3, /device:TPU:1, one launch (start us, length us, event | category | flops | bytes accessed | tf_op | source)
XLA Modules:
  0.0 82.6 jit_solution(339493771460255539)
XLA Ops:
  0.6 80.0 %shard_map.77 = (bf16[128,1024]{1,0:T(8,128)(2,1)}, bf16[128,1024]{1,0:T(8,128)(2,1)}) custom-call(bf16[128,1024]{1,0:T(8,128)(2,1)} %tok_hbm.1, bf16[128,1024]{1,0:T(8,128)(2,1)} %cot_hbm.1, bf16[1024,3072]{1,0:T(8,128)(2,1)} %wqkv_hbm.1, bf16[1024,1024]{1,0:T(8,128)(2,1)} %wout_hbm.1, f32[7,1024]{1,0:T(8,128)} %convk_hbm.1, s32[32]{0:T(128)} %lens_hbm.1), custom_call_target="tpu_custom_call" | custom-call | tf_op jit(solution)/shard_map/pallas_call | solution.py:650
  80.6 1.8 %shard_map.78 = (bf16[128,1024]{1,0:T(8,128)(2,1)}, bf16[128,1024]{1,0:T(8,128)(2,1)}) custom-call(bf16[128,1024]{1,0:T(8,128)(2,1)} %get-tuple-element.4.a_hbm, bf16[128,1024]{1,0:T(8,128)(2,1)} %get-tuple-element.5.b_hbm), custom_call_target="tpu_custom_call" | custom-call | tf_op jit(solution)/shard_map/pallas_call | solution.py:660

commit v4 on v3

--- a/solution.py
+++ b/solution.py
@@ -277,15 +277,6 @@
         if d:
             give_q(0, d)
     forward_q(0, 0)
-    for d in (2, 1, 3):
-        give_kv(1, d)
-    for d in (2, 1, 3):
-        give_q(1, d)
-    for d in ways:
-        kv_sends[0, d].wait_recv()
-        forward(0, d)
-    forward(1, 0)
-    forward_q(1, 0)
 
     loads[6].wait()
     loads[7].wait()
@@ -293,14 +284,15 @@
         block = nt(cot[...], wout[columns(peer_at[d]), :]).astype(BF16)
         if d:
             ds_[d] = block
-            d_sends[d] = send(ds_.at[d], do.at[0, mine, :], s_d.at[d], r_d.at[d], (c, peer_at[d]))
         else:
             do[0, mine, :] = block
+    for d in ways:
+        kv_sends[0, d].wait_recv()
+        forward(0, d)
     ot[...] = jnp.zeros_like(ot)
     tot[...] = jnp.zeros_like(tot)
     dqt[...] = jnp.zeros_like(dqt)
     dkv[...] = jnp.zeros_like(dkv)
-
     lane = lax.broadcasted_iota(I32, (8, seq), 1)
     for qi, shard in ((0, c), (1, ahead)):
         pos = shard * seq + lane
@@ -312,6 +304,14 @@
     for d in ways:
         q_sends[0, d].wait_recv()
         forward_q(0, d)
+    for d in (2, 1, 3):
+        give_kv(1, d)
+    forward(1, 0)
+    for d in (2, 1, 3):
+        give_q(1, d)
+    forward_q(1, 0)
+    for d in (2, 1, 3):
+        d_sends[d] = send(ds_.at[d], do.at[0, mine, :], s_d.at[d], r_d.at[d], (c, peer_at[d]))
 
     def split_pair(block, dst, qi, hp):
         block = block.astype(F32)

time: 82.7 us -> 82 us (level)
  no operation moved by 1% of the time
where the time goes in v4:
time: 82 us; the launch traced here: 81.9 us
  Pallas kernels  81.1 us (99%)
    pallas_call x1, Pallas kernels, on_device(): pl.pallas_call(functools.partial(layer_kernel, lax.axis_size('ctx')), out...  79.4 us
    pallas_call x1, Pallas kernels, on_device(): pl.pallas_call(settle_kernel, out_shape=(out, out), in_specs=[anywhere] *...  1.77 us

profile of v4, /device:TPU:1, one launch (start us, length us, event | category | flops | bytes accessed | tf_op | source)
XLA Modules:
  0.0 81.9 jit_solution(536708425379775305)
XLA Ops:
  0.6 79.4 %shard_map.77 = (bf16[128,1024]{1,0:T(8,128)(2,1)}, bf16[128,1024]{1,0:T(8,128)(2,1)}) custom-call(bf16[128,1024]{1,0:T(8,128)(2,1)} %tok_hbm.1, bf16[128,1024]{1,0:T(8,128)(2,1)} %cot_hbm.1, bf16[1024,3072]{1,0:T(8,128)(2,1)} %wqkv_hbm.1, bf16[1024,1024]{1,0:T(8,128)(2,1)} %wout_hbm.1, f32[7,1024]{1,0:T(8,128)} %convk_hbm.1, s32[32]{0:T(128)} %lens_hbm.1), custom_call_target="tpu_custom_call" | custom-call | tf_op jit(solution)/shard_map/pallas_call | solution.py:650
  80.0 1.8 %shard_map.78 = (bf16[128,1024]{1,0:T(8,128)(2,1)}, bf16[128,1024]{1,0:T(8,128)(2,1)}) custom-call(bf16[128,1024]{1,0:T(8,128)(2,1)} %get-tuple-element.4.a_hbm, bf16[128,1024]{1,0:T(8,128)(2,1)} %get-tuple-element.5.b_hbm), custom_call_target="tpu_custom_call" | custom-call | tf_op jit(solution)/shard_map/pallas_call | solution.py:660

commit v5 on v4

--- a/solution.py
+++ b/solution.py
@@ -482,7 +482,9 @@
                 )
 
     cx_sends = {}
-    for hp in (0, 1):
+    st_sends = [None, None]
+
+    def context_of(hp):
         for copy in of_sends[hp]:
             copy.wait_recv()
         d_turned = do[0, :, hp * 128 : hp * 128 + 128].astype(F32).T
@@ -495,7 +497,7 @@
             st_s[hp, s : s + 1, :] = 1.0 / total
             st_s[hp, 4 + s : 5 + s, :] = jnp.sum(d_turned[head_rows, :] * context, axis=0, keepdims=True)
         stat[0, hp] = st_s[hp]
-        st = send(st_s.at[hp], stat.at[1, hp], s_f.at[5 + hp], r_f.at[5 + hp], (behind, x))
+        st_sends[hp] = send(st_s.at[hp], stat.at[1, hp], s_f.at[5 + hp], r_f.at[5 + hp], (behind, x))
         lanes = pl.ds(hp * 128, 128)
         for d in (2, 1, 3, 0):
             block = ctxt[:, row_block(peer_at[d])].T.astype(BF16)
@@ -508,6 +510,11 @@
             else:
                 cx[0, :, lanes] = block
 
+    context_of(0)
+    for hp in (0, 1):
+        if hp == 0:
+            for lower in LOWER:
+                grads(0, 0, OWN, 0, *lower)
         for part in (0, 1):
             k0 = part * kc
             keys_at = pl.ds(k0, kc)
@@ -520,7 +527,7 @@
             lax.fori_loop(0, 2, near_grads, 0)
             pass_back()
             if part == 0:
-                st.wait_recv()
+                st_sends[hp].wait_recv()
             grads(4, far, PREVX + core, hp, k0, 0, seq)
             pp_s[hp, keys_at, :] = dkv[PREVX, hp, keys_at, :].astype(BF16)
             ppg = send(
@@ -541,10 +548,12 @@
                     dqf_s.at[hp], dqf_r.at[hp], s_gr.at[12 + hp], r_gr.at[12 + hp], (ahead, x)
                 )
                 if hp == 1:
+                    grads(0, 0, OWN, 1, *LOWER[1])
+                    pass_back()
                     give(0)
-                grads(0, 0, OWN, hp, *LOWER[1])
-                pass_back()
-                grads(0, 0, OWN, hp, *LOWER[0])
+                    grads(0, 0, OWN, 1, *LOWER[0])
+            elif hp == 0:
+                context_of(1)
     give(1)
 
     def take(group, d):

time: 82 us -> 78.8 us (0.961)
  Pallas kernels: 81.1 us -> 77.9 us
    pallas_call x1, Pallas kernels: 79.4 us -> 76.2 us  [on_device(): pl.pallas_call(functools.partial(layer_kernel, lax.axis_size('ctx')), out...]
where the time goes in v5:
time: 78.8 us; the launch traced here: 78.7 us
  Pallas kernels  77.9 us (99%)
  between operations  0.8 us (1%)
    pallas_call x1, Pallas kernels, on_device(): pl.pallas_call(functools.partial(layer_kernel, lax.axis_size('ctx')), out...  76.2 us
    pallas_call x1, Pallas kernels, on_device(): pl.pallas_call(settle_kernel, out_shape=(out, out), in_specs=[anywhere] *...  1.77 us

profile of v5, /device:TPU:1, one launch (start us, length us, event | category | flops | bytes accessed | tf_op | source)
XLA Modules:
  0.0 78.7 jit_solution(4195028497140996281)
XLA Ops:
  0.6 76.2 %shard_map.77 = (bf16[128,1024]{1,0:T(8,128)(2,1)}, bf16[128,1024]{1,0:T(8,128)(2,1)}) custom-call(bf16[128,1024]{1,0:T(8,128)(2,1)} %tok_hbm.1, bf16[128,1024]{1,0:T(8,128)(2,1)} %cot_hbm.1, bf16[1024,3072]{1,0:T(8,128)(2,1)} %wqkv_hbm.1, bf16[1024,1024]{1,0:T(8,128)(2,1)} %wout_hbm.1, f32[7,1024]{1,0:T(8,128)} %convk_hbm.1, s32[32]{0:T(128)} %lens_hbm.1), custom_call_target="tpu_custom_call" | custom-call | tf_op jit(solution)/shard_map/pallas_call | solution.py:659
  76.8 1.8 %shard_map.78 = (bf16[128,1024]{1,0:T(8,128)(2,1)}, bf16[128,1024]{1,0:T(8,128)(2,1)}) custom-call(bf16[128,1024]{1,0:T(8,128)(2,1)} %get-tuple-element.4.a_hbm, bf16[128,1024]{1,0:T(8,128)(2,1)} %get-tuple-element.5.b_hbm), custom_call_target="tpu_custom_call" | custom-call | tf_op jit(solution)/shard_map/pallas_call | solution.py:669

commit v6 on v5

--- a/solution.py
+++ b/solution.py
@@ -554,8 +554,6 @@
                     grads(0, 0, OWN, 1, *LOWER[0])
             elif hp == 0:
                 context_of(1)
-    give(1)
-
     def take(group, d):
         if d:
             g_sends[group, d].wait_recv()
@@ -570,6 +568,7 @@
             cx_sends[hp, d].wait_recv()
         acc = acc + nn(cx[d], wout[columns(source[d]), :])
     att_out[...] = acc.astype(BF16)
+    give(1)
     gacc[...] = take(0, 0) + take(1, 0)
     for d in ways:
         gacc[...] += take(0, d)

time: 78.8 us -> 78.7 us (level)
  no operation moved by 1% of the time
where the time goes in v6:
time: 78.7 us; the launch traced here: 78.6 us
  Pallas kernels  77.8 us (99%)
  between operations  0.8 us (1%)
    pallas_call x1, Pallas kernels, on_device(): pl.pallas_call(functools.partial(layer_kernel, lax.axis_size('ctx')), out...  76 us
    pallas_call x1, Pallas kernels, on_device(): pl.pallas_call(settle_kernel, out_shape=(out, out), in_specs=[anywhere] *...  1.77 us

profile of v6, /device:TPU:1, one launch (start us, length us, event | category | flops | bytes accessed | tf_op | source)
XLA Modules:
  0.0 78.6 jit_solution(119065835705226181)
XLA Ops:
  0.6 76.0 %shard_map.77 = (bf16[128,1024]{1,0:T(8,128)(2,1)}, bf16[128,1024]{1,0:T(8,128)(2,1)}) custom-call(bf16[128,1024]{1,0:T(8,128)(2,1)} %tok_hbm.1, bf16[128,1024]{1,0:T(8,128)(2,1)} %cot_hbm.1, bf16[1024,3072]{1,0:T(8,128)(2,1)} %wqkv_hbm.1, bf16[1024,1024]{1,0:T(8,128)(2,1)} %wout_hbm.1, f32[7,1024]{1,0:T(8,128)} %convk_hbm.1, s32[32]{0:T(128)} %lens_hbm.1), custom_call_target="tpu_custom_call" | custom-call | tf_op jit(solution)/shard_map/pallas_call | solution.py:658
  76.6 1.8 %shard_map.78 = (bf16[128,1024]{1,0:T(8,128)(2,1)}, bf16[128,1024]{1,0:T(8,128)(2,1)}) custom-call(bf16[128,1024]{1,0:T(8,128)(2,1)} %get-tuple-element.4.a_hbm, bf16[128,1024]{1,0:T(8,128)(2,1)} %get-tuple-element.5.b_hbm), custom_call_target="tpu_custom_call" | custom-call | tf_op jit(solution)/shard_map/pallas_call | solution.py:668
